TPU v7x, 32 devices: a whole 2x2x4 slice. The times are simulated.
32 devices in a mesh: groups: 2 (over x), rows: 16 (over z, y, core).
Axes of the slice: x: 2, y: 2, z: 4, core: 2. Of those that a mesh axis runs over, the one named last changes fastest.
Arguments:
- tap_two: bfloat16 [6144, 1024], P(('groups', 'rows')), parts along dimension 0, may hold values from -6 to 6
- coarse_path: bfloat16 [6144, 256], P(('groups', 'rows')), parts along dimension 0, may hold values from -6 to 6
- proj_weight: bfloat16 [1024, 512], replicated, may hold values from -0.1875 to 0.1875
- proj_bias: float32 [512], replicated, may hold values from -3 to 3
- lift_weight: bfloat16 [512, 2048], replicated, may hold values from -0.25 to 0.25
- lift_bias: float32 [512], replicated, may hold values from -3 to 3
- merge_weight: bfloat16 [4608, 256], replicated, may hold values from -0.09375 to 0.09375
- out_weight: bfloat16 [256, 256], replicated, may hold values from -0.375 to 0.375
- out_bias: float32 [256], replicated, may hold values from -3 to 3
- first_inner_w: bfloat16 [2304, 256], replicated, may hold values from -0.125 to 0.125
- first_inner_b: float32 [256], replicated, may hold values from -3 to 3
- first_outer_w: bfloat16 [2304, 256], replicated, may hold values from -0.125 to 0.125
- first_outer_b: float32 [256], replicated, may hold values from -3 to 3
- second_inner_w: bfloat16 [2304, 256], replicated, may hold values from -0.125 to 0.125
- second_inner_b: float32 [256], replicated, may hold values from -3 to 3
- second_outer_w: bfloat16 [2304, 256], replicated, may hold values from -0.125 to 0.125
- second_outer_b: float32 [256], replicated, may hold values from -3 to 3
Outputs:
- united: bfloat16 [64, 384, 256], P(('groups', 'rows')), parts along dimension 0
There are 2 independent parts, one for each index of `groups`. A program takes and returns all parts, laid end to end along the dimension named above; an argument that names none is the same for every part. Nothing has to cross between parts.
All inputs are finite; a program needn't handle non-finite values.
Results may differ from a plain program's by a relative error of at most 0.0075.
Values may be sent and summed in bfloat16 or wider, within the bound.
No kernel may reach another device: no remote copies, remote signals or barrier semaphores. Data moves between devices by JAX's collectives and lax.ppermute only.
A program may use at most 64 MiB of HBM per device.

v0:
```python
import jax
import jax.numpy as jnp
from jax import lax
from jax.sharding import PartitionSpec as P

GW = 192


def padded(block, sides, width):
    for axis, dim in sides:
        count = lax.axis_size(axis)
        forward = [(i, i + 1) for i in range(count - 1)]
        backward = [(target, source) for source, target in forward]
        low = lax.ppermute(
            lax.slice_in_dim(block, block.shape[dim] - width, None, axis=dim), axis, forward
        )
        high = lax.ppermute(lax.slice_in_dim(block, 0, width, axis=dim), axis, backward)
        block = jnp.concatenate([low, block, high], axis=dim)
    return block


def stripe_rim(inside):
    grown = padded(inside, (("rows", 0),), 1)
    return jnp.pad(grown, ((0, 0), (1, 1), (0, 0)))


def clamp_edges(grown, edges):
    at_top, at_bottom, at_left, at_right = edges
    first_row = jnp.where(at_top, grown[1:2], grown[:1])
    last_row = jnp.where(at_bottom, grown[-2:-1], grown[-1:])
    grown = jnp.concatenate([first_row, grown[1:-1], last_row], axis=0)
    first_col = jnp.where(at_left, grown[:, 1:2], grown[:, :1])
    last_col = jnp.where(at_right, grown[:, -2:-1], grown[:, -1:])
    return jnp.concatenate([first_col, grown[:, 1:-1], last_col], axis=1)


def enlarge(grown):
    upper = 0.25 * grown[:-2] + 0.75 * grown[1:-1]
    lower = 0.75 * grown[1:-1] + 0.25 * grown[2:]

    def sideways(band):
        return (
            0.25 * band[:, :-2] + 0.75 * band[:, 1:-1],
            0.75 * band[:, 1:-1] + 0.25 * band[:, 2:],
        )

    upper_left, upper_right = sideways(upper)
    lower_left, lower_right = sideways(lower)
    top_pair = jnp.stack([upper_left, upper_right], axis=2)
    bottom_pair = jnp.stack([lower_left, lower_right], axis=2)
    joined = jnp.stack([top_pair, bottom_pair], axis=1)
    height, across, channels = upper_left.shape
    return joined.reshape(2 * height, 2 * across, channels)


def conv_block(grown, weight):
    height = grown.shape[0] - 2
    across = grown.shape[1] - 2
    channels = grown.shape[2]
    columns = jnp.concatenate(
        [
            grown[offset_row : offset_row + height, offset_col : offset_col + across]
            for offset_row in range(3)
            for offset_col in range(3)
        ],
        axis=-1,
    )
    result = jnp.dot(
        columns.reshape(height * across, 9 * channels), weight, preferred_element_type=jnp.float32
    )
    return result.reshape(height, across, weight.shape[1])


def residual_unit(value, inner_w, inner_b, outer_w, outer_b, extra, extend):
    first_pass = conv_block(extend(jnp.maximum(value, 0)), inner_w) + inner_b
    inner = jnp.maximum(first_pass, 0.0).astype(jnp.bfloat16)
    return conv_block(extend(inner), outer_w) + outer_b + value.astype(jnp.float32) + extra


def body(
    tap_two,
    coarse_path,
    proj_weight,
    proj_bias,
    lift_weight,
    lift_bias,
    merge_weight,
    out_weight,
    out_bias,
    first_inner_w,
    first_inner_b,
    first_outer_w,
    first_outer_b,
    second_inner_w,
    second_inner_b,
    second_outer_w,
    second_outer_b,
):
    stripe_rows = tap_two.shape[0] // GW
    tokens_grid = tap_two.reshape(stripe_rows, GW, tap_two.shape[1])
    coarse_grid = coarse_path.reshape(stripe_rows, GW, coarse_path.shape[1])
    position = lax.axis_index("rows")
    devices_here = lax.axis_size("rows")
    edges = (position == 0, position == devices_here - 1, True, True)
    height, across, channels = tokens_grid.shape
    result = (
        jnp.dot(
            tokens_grid.reshape(height * across, channels),
            proj_weight,
            preferred_element_type=jnp.float32,
        )
        + proj_bias
    )
    features = result.astype(jnp.bfloat16).reshape(height, across, proj_weight.shape[1])
    height, across, channels = features.shape
    lifted = jnp.dot(
        features.reshape(height * across, channels), lift_weight, preferred_element_type=jnp.float32
    )
    lifted = lifted.reshape(height, across, 2, 2, channels) + lift_bias
    widened = (
        lifted.transpose(0, 2, 1, 3, 4)
        .reshape(2 * height, 2 * across, channels)
        .astype(jnp.bfloat16)
    )
    reassembled = conv_block(stripe_rim(widened), merge_weight).astype(jnp.bfloat16)
    spread = enlarge(clamp_edges(stripe_rim(coarse_grid).astype(jnp.float32), edges)).astype(
        jnp.bfloat16
    )
    fine_rows, fine_cols, fine_channels = spread.shape
    carried = (
        jnp.dot(
            spread.reshape(fine_rows * fine_cols, fine_channels),
            out_weight,
            preferred_element_type=jnp.float32,
        )
        + out_bias
    )
    carried = carried.reshape(fine_rows, fine_cols, out_weight.shape[1])
    merged = residual_unit(
        reassembled, first_inner_w, first_inner_b, first_outer_w, first_outer_b, carried, stripe_rim
    ).astype(jnp.bfloat16)
    united = residual_unit(
        merged, second_inner_w, second_inner_b, second_outer_w, second_outer_b, 0.0, stripe_rim
    ).astype(jnp.bfloat16)
    return united


def solution(mesh):
    return jax.shard_map(
        body,
        mesh=mesh,
        in_specs=(
            P(("groups", "rows"), None),
            P(("groups", "rows"), None),
            P(),
            P(),
            P(),
            P(),
            P(),
            P(),
            P(),
            P(),
            P(),
            P(),
            P(),
            P(),
            P(),
            P(),
            P(),
        ),
        out_specs=P(("groups", "rows"), None, None),
        check_vma=False,
    )
```

profile of v0, /device:TPU:9, one launch (start us, length us, event | category | flops | bytes accessed | tf_op | source)
XLA Modules:
  0.0 94.8 jit_solution(5978575095199426015)
XLA Ops:
  0.0 3.8 %collective-permute-start.6 = (bf16[1,192,256]{2,1,0:T(8,128)(2,1)}, bf16[1,192,256]{2,1,0:T(8,128)(2,1)}, u32[]{:S(2)}, u32[]{:S(2)}) collective-permute-start(bf16[1,192,256]{2,1,0:T(8,128)(2,1)} %bitcast.50), channel_id=1, source_target_pairs={{0,1},{1,2},{2,3},{3,4},{4,5},{5,6},{6,7},{7,8},{8,9},{9,10},{10,1... | collective-permute-start | bytes 294920 | tf_op jit(solution)/shard_map/ppermute | solution.py:14
  3.8 1.9 %collective-permute-start.7 = (bf16[1,192,256]{2,1,0:T(8,128)(2,1)}, bf16[1,192,256]{2,1,0:T(8,128)(2,1)}, u32[]{:S(2)}, u32[]{:S(2)}) collective-permute-start(bf16[1,192,256]{2,1,0:T(8,128)(2,1)} %bitcast.51), channel_id=1, source_target_pairs={{1,0},{2,1},{3,2},{4,3},{5,4},{6,5},{7,6},{8,7},{9,8},{10,9},{11,1... | collective-permute-start | bytes 294920 | tf_op jit(solution)/shard_map/ppermute | solution.py:17
  5.8 4.1 %fusion.26 = f32[192,2048]{1,0:T(8,128)} fusion(bf16[512,2048]{1,0:T(8,128)(2,1)} %param.21, bf16[192,1024]{1,0:T(8,128)(2,1)} %param.17, bf16[1024,512]{1,0:T(8,128)(2,1)} %param.19, f32[512]{0:T(512)} %param.20), kind=kOutput, calls=%fused_computation.35 | convolution fusion | flops 604176384 | bytes 5113856 | tf_op jit(solution)/shard_map/dot_general | solution.py:116
  9.9 3.4 %reshape.64 = f32[1,192,2,2,512]{4,3,2,1,0:T(2,128)} reshape(f32[192,2048]{1,0:T(8,128)} %fusion.26) | data formatting | bytes 3145728 | tf_op jit(solution)/shard_map/reshape | solution.py:119
  13.3 2.0 %fusion.42 = bf16[1,2,192,2,512]{4,3,1,2,0:T(2,128)(2,1)S(1)} fusion(f32[1,192,2,2,512]{4,3,2,1,0:T(2,128)} %reshape.64, f32[512]{0:T(512)S(1)} %copy-done.6), kind=kLoop, calls=%fused_computation.55 | loop fusion | flops 786432 | bytes 2361344 | tf_op jit(solution)/shard_map/convert_element_type | solution.py:123
  16.6 1.9 %slice.239 = bf16[1,384,512]{2,1,0:T(8,128)(2,1)} reshape(bf16[1,1,192,2,512]{4,3,1,2,0:T(2,128)(2,1)} %get-tuple-element.5) | data formatting | bytes 786432 | tf_op jit(solution)/shard_map/slice | solution.py:15
  18.5 3.6 %collective-permute-start = (bf16[1,384,512]{2,1,0:T(8,128)(2,1)}, bf16[1,384,512]{2,1,0:T(8,128)(2,1)}, u32[]{:S(2)}, u32[]{:S(2)}) collective-permute-start(bf16[1,384,512]{2,1,0:T(8,128)(2,1)} %slice.239), channel_id=1, source_target_pairs={{0,1},{1,2},{2,3},{3,4},{4,5},{5,6},{6,7},{7,8},{8,9},{9,10},{10,1... | collective-permute-start | bytes 1179656 | tf_op jit(solution)/shard_map/ppermute | solution.py:14
  23.0 1.9 %collective-permute-start.1 = (bf16[1,384,512]{2,1,0:T(8,128)(2,1)}, bf16[1,384,512]{2,1,0:T(8,128)(2,1)S(1)}, u32[]{:S(2)}, u32[]{:S(2)}) collective-permute-start(bf16[1,384,512]{2,1,0:T(8,128)(2,1)} %slice.241), channel_id=1, source_target_pairs={{1,0},{2,1},{3,2},{4,3},{5,4},{6,5},{7,6},{8,7},{9,8},{10,9},{11,1... | collective-permute-start | bytes 1179656 | tf_op jit(solution)/shard_map/ppermute | solution.py:17
  26.4 2.3 %convert_element_type.53 = bf16[2,384,512]{2,1,0:T(8,128)(2,1)S(1)} reshape(bf16[1,2,192,2,512]{4,3,2,1,0:T(2,128)(2,1)} %copy.19) | data formatting | bytes 1572864 | tf_op jit(solution)/shard_map/convert_element_type | solution.py:123
  31.7 1.7 %stack.36 = bf16[1,384,256]{2,1,0:T(8,128)(2,1)} reshape(bf16[1,192,2,256]{3,2,1,0:T(2,128)(2,1)} %copy.20) | data formatting | bytes 393216 | tf_op jit(solution)/shard_map/stack | solution.py:51
  37.1 2.7 %broadcast_maximum_fusion.1 = (bf16[2,384,256]{2,1,0:T(8,128)(2,1)S(1)}, bf16[2,384,256]{2,1,0:T(8,128)(2,1)}) fusion(bf16[2,384,4608]{2,1,0:T(8,128)(2,1)S(1)} %slice_dynamic-update-slice_fusion, bf16[4608,256]{1,0:T(8,128)(2,1)S(1)} %copy-done), kind=kOutput, calls=%fused_computation.147 | convolution fusion | flops 1812332544 | bytes 10223616 | tf_op jit(solution)/shard_map/dot_general | solution.py:68
  40.6 3.3 %collective-permute-start.2 = (bf16[1,384,256]{2,1,0:T(8,128)(2,1)}, bf16[1,384,256]{2,1,0:T(8,128)(2,1)}, u32[]{:S(2)}, u32[]{:S(2)}) collective-permute-start(bf16[1,384,256]{2,1,0:T(8,128)(2,1)} %get-tuple-element.18), channel_id=1, source_target_pairs={{0,1},{1,2},{2,3},{3,4},{4,5},{5,6},{6,7},{7,8},{8,9},{9,10},{10,1... | collective-permute-start | bytes 589832 | tf_op jit(solution)/shard_map/ppermute | solution.py:14
  43.9 2.6 %collective-permute-start.3 = (bf16[1,384,256]{2,1,0:T(8,128)(2,1)}, bf16[1,384,256]{2,1,0:T(8,128)(2,1)S(1)}, u32[]{:S(2)}, u32[]{:S(2)}) collective-permute-start(bf16[1,384,256]{2,1,0:T(8,128)(2,1)} %get-tuple-element.19), channel_id=1, source_target_pairs={{1,0},{2,1},{3,2},{4,3},{5,4},{6,5},{7,6},{8,7},{9,8},{10,9},{11,1... | collective-permute-start | bytes 589832 | tf_op jit(solution)/shard_map/ppermute | solution.py:17
  46.9 5.2 %collective-permute-done.3 = bf16[1,384,256]{2,1,0:T(8,128)(2,1)S(1)} collective-permute-done((bf16[1,384,256]{2,1,0:T(8,128)(2,1)}, bf16[1,384,256]{2,1,0:T(8,128)(2,1)S(1)}, u32[]{:S(2)}, u32[]{:S(2)}) %collective-permute-start.3) | collective-permute-done | bytes 196640 | tf_op jit(solution)/shard_map/ppermute | solution.py:17
  56.1 1.9 %collective-permute-start.4 = (bf16[1,384,256]{2,1,0:T(8,128)(2,1)S(1)}, bf16[1,384,256]{2,1,0:T(8,128)(2,1)S(1)}, u32[]{:S(2)}, u32[]{:S(2)}) collective-permute-start(bf16[1,384,256]{2,1,0:T(8,128)(2,1)S(1)} %get-tuple-element.16), channel_id=1, source_target_pairs={{0,1},{1,2},{2,3},{3,4},{4,5},{5,6},{6,7},{7,8},{8,9},{9,10},{10,1... | collective-permute-start | bytes 589832 | tf_op jit(solution)/shard_map/ppermute | solution.py:14
  58.0 2.6 %collective-permute-start.5 = (bf16[1,384,256]{2,1,0:T(8,128)(2,1)S(1)}, bf16[1,384,256]{2,1,0:T(8,128)(2,1)S(1)}, u32[]{:S(2)}, u32[]{:S(2)}) collective-permute-start(bf16[1,384,256]{2,1,0:T(8,128)(2,1)S(1)} %get-tuple-element.17), channel_id=1, source_target_pairs={{1,0},{2,1},{3,2},{4,3},{5,4},{6,5},{7,6},{8,7},{9,8},{10,9},{11,1... | collective-permute-start | bytes 589832 | tf_op jit(solution)/shard_map/ppermute | solution.py:17
  60.9 5.6 %collective-permute-done.5 = bf16[1,384,256]{2,1,0:T(8,128)(2,1)S(1)} collective-permute-done((bf16[1,384,256]{2,1,0:T(8,128)(2,1)S(1)}, bf16[1,384,256]{2,1,0:T(8,128)(2,1)S(1)}, u32[]{:S(2)}, u32[]{:S(2)}) %collective-permute-start.5) | collective-permute-done | bytes 196640 | tf_op jit(solution)/shard_map/ppermute | solution.py:17
  69.2 1.9 %collective-permute-start.8 = (bf16[1,384,256]{2,1,0:T(8,128)(2,1)S(1)}, bf16[1,384,256]{2,1,0:T(8,128)(2,1)S(1)}, u32[]{:S(2)}, u32[]{:S(2)}) collective-permute-start(bf16[1,384,256]{2,1,0:T(8,128)(2,1)S(1)} %get-tuple-element.14), channel_id=1, source_target_pairs={{0,1},{1,2},{2,3},{3,4},{4,5},{5,6},{6,7},{7,8},{8,9},{9,10},{10,1... | collective-permute-start | bytes 589832 | tf_op jit(solution)/shard_map/ppermute | solution.py:14
  71.1 2.4 %collective-permute-start.9 = (bf16[1,384,256]{2,1,0:T(8,128)(2,1)S(1)}, bf16[1,384,256]{2,1,0:T(8,128)(2,1)S(1)}, u32[]{:S(2)}, u32[]{:S(2)}) collective-permute-start(bf16[1,384,256]{2,1,0:T(8,128)(2,1)S(1)} %get-tuple-element.15), channel_id=1, source_target_pairs={{1,0},{2,1},{3,2},{4,3},{5,4},{6,5},{7,6},{8,7},{9,8},{10,9},{11,1... | collective-permute-start | bytes 589832 | tf_op jit(solution)/shard_map/ppermute | solution.py:17
  73.7 5.3 %collective-permute-done.9 = bf16[1,384,256]{2,1,0:T(8,128)(2,1)S(1)} collective-permute-done((bf16[1,384,256]{2,1,0:T(8,128)(2,1)S(1)}, bf16[1,384,256]{2,1,0:T(8,128)(2,1)S(1)}, u32[]{:S(2)}, u32[]{:S(2)}) %collective-permute-start.9) | collective-permute-done | bytes 196640 | tf_op jit(solution)/shard_map/ppermute | solution.py:17
  81.6 1.9 %collective-permute-start.10 = (bf16[1,384,256]{2,1,0:T(8,128)(2,1)S(1)}, bf16[1,384,256]{2,1,0:T(8,128)(2,1)S(1)}, u32[]{:S(2)}, u32[]{:S(2)}) collective-permute-start(bf16[1,384,256]{2,1,0:T(8,128)(2,1)S(1)} %get-tuple-element.12), channel_id=1, source_target_pairs={{0,1},{1,2},{2,3},{3,4},{4,5},{5,6},{6,7},{7,8},{8,9},{9,10},{10,1... | collective-permute-start | bytes 589832 | tf_op jit(solution)/shard_map/ppermute | solution.py:14
  83.5 2.4 %collective-permute-start.11 = (bf16[1,384,256]{2,1,0:T(8,128)(2,1)S(1)}, bf16[1,384,256]{2,1,0:T(8,128)(2,1)S(1)}, u32[]{:S(2)}, u32[]{:S(2)}) collective-permute-start(bf16[1,384,256]{2,1,0:T(8,128)(2,1)S(1)} %get-tuple-element.13), channel_id=1, source_target_pairs={{1,0},{2,1},{3,2},{4,3},{5,4},{6,5},{7,6},{8,7},{9,8},{10,9},{11,1... | collective-permute-start | bytes 589832 | tf_op jit(solution)/shard_map/ppermute | solution.py:17
  86.1 5.3 %collective-permute-done.11 = bf16[1,384,256]{2,1,0:T(8,128)(2,1)S(1)} collective-permute-done((bf16[1,384,256]{2,1,0:T(8,128)(2,1)S(1)}, bf16[1,384,256]{2,1,0:T(8,128)(2,1)S(1)}, u32[]{:S(2)}, u32[]{:S(2)}) %collective-permute-start.11) | collective-permute-done | bytes 196640 | tf_op jit(solution)/shard_map/ppermute | solution.py:17
  92.9 1.8 %fusion.20 = bf16[2,384,256]{2,1,0:T(8,128)(2,1)} fusion(bf16[2,384,2304]{2,1,0:T(8,128)(2,1)S(1)} %slice_dynamic-update-slice_fusion.6, bf16[2304,256]{1,0:T(8,128)(2,1)S(1)} %copy-done.11, bf16[2,384,256]{2,1,0:T(8,128)(2,1)S(1)} %get-tuple-element.27, f32[256]{0:T(256)S(1)} %copy-done.15), kind=kOutput, calls=%fused_computation.28 | convolution fusion | flops 906756096 | bytes 5506048 | tf_op jit(solution)/shard_map/dot_general | solution.py:68
  (114 shorter events, 22.2 us)
Async XLA Ops:
  0.0 37.0 %copy-start = (bf16[4608,256]{1,0:T(8,128)(2,1)S(1)}, bf16[4608,256]{1,0:T(8,128)(2,1)}, u32[]{:S(2)}) copy-start(bf16[4608,256]{1,0:T(8,128)(2,1)} %param.23) | copy-start | bytes 7077892
  0.0 13.3 %copy-start.6 = (f32[512]{0:T(512)S(1)}, f32[512]{0:T(512)}, u32[]{:S(2)}) copy-start(f32[512]{0:T(512)} %param.22) | copy-start | bytes 6148
  0.0 28.6 %collective-permute-start.6 = (bf16[1,192,256]{2,1,0:T(8,128)(2,1)}, bf16[1,192,256]{2,1,0:T(8,128)(2,1)}, u32[]{:S(2)}, u32[]{:S(2)}) collective-permute-start(bf16[1,192,256]{2,1,0:T(8,128)(2,1)} %bitcast.50), channel_id=1, source_target_pairs={{0,1},{1,2},{2,3},{3,4},{4,5},{5,6},{6,7},{7,8},{8,9},{9,10},{10,1... | collective-permute-start | bytes 294920 | tf_op jit(solution)/shard_map/ppermute | solution.py:14
  3.8 24.8 %collective-permute-start.7 = (bf16[1,192,256]{2,1,0:T(8,128)(2,1)}, bf16[1,192,256]{2,1,0:T(8,128)(2,1)}, u32[]{:S(2)}, u32[]{:S(2)}) collective-permute-start(bf16[1,192,256]{2,1,0:T(8,128)(2,1)} %bitcast.51), channel_id=1, source_target_pairs={{1,0},{2,1},{3,2},{4,3},{5,4},{6,5},{7,6},{8,7},{9,8},{10,9},{11,1... | collective-permute-start | bytes 294920 | tf_op jit(solution)/shard_map/ppermute | solution.py:17
  18.5 14.9 %collective-permute-start = (bf16[1,384,512]{2,1,0:T(8,128)(2,1)}, bf16[1,384,512]{2,1,0:T(8,128)(2,1)}, u32[]{:S(2)}, u32[]{:S(2)}) collective-permute-start(bf16[1,384,512]{2,1,0:T(8,128)(2,1)} %slice.239), channel_id=1, source_target_pairs={{0,1},{1,2},{2,3},{3,4},{4,5},{5,6},{6,7},{7,8},{8,9},{9,10},{10,1... | collective-permute-start | bytes 1179656 | tf_op jit(solution)/shard_map/ppermute | solution.py:14
  23.0 10.7 %collective-permute-start.1 = (bf16[1,384,512]{2,1,0:T(8,128)(2,1)}, bf16[1,384,512]{2,1,0:T(8,128)(2,1)S(1)}, u32[]{:S(2)}, u32[]{:S(2)}) collective-permute-start(bf16[1,384,512]{2,1,0:T(8,128)(2,1)} %slice.241), channel_id=1, source_target_pairs={{1,0},{2,1},{3,2},{4,3},{5,4},{6,5},{7,6},{8,7},{9,8},{10,9},{11,1... | collective-permute-start | bytes 1179656 | tf_op jit(solution)/shard_map/ppermute | solution.py:17
  37.0 9.5 %copy-start.3 = (bf16[1,192,1,256]{3,1,2,0:T(8,128)(2,1)S(1)}, bf16[1,192,1,256]{3,1,2,0:T(8,128)(2,1)}, u32[]{:S(2)}) copy-start(bf16[1,192,1,256]{3,1,2,0:T(8,128)(2,1)} %get-tuple-element.28) | copy-start | bytes 294916
  37.0 9.5 %copy-start.4 = (bf16[1,192,1,256]{3,1,2,0:T(8,128)(2,1)S(1)}, bf16[1,192,1,256]{3,1,2,0:T(8,128)(2,1)}, u32[]{:S(2)}) copy-start(bf16[1,192,1,256]{3,1,2,0:T(8,128)(2,1)} %get-tuple-element.29) | copy-start | bytes 294916
  37.0 9.8 %copy-start.1 = (bf16[1,384,256]{2,1,0:T(8,128)(2,1)S(1)}, bf16[1,384,256]{2,1,0:T(8,128)(2,1)}, u32[]{:S(2)}) copy-start(bf16[1,384,256]{2,1,0:T(8,128)(2,1)} %stack.36) | copy-start | bytes 589828
  40.6 6.4 %collective-permute-start.2 = (bf16[1,384,256]{2,1,0:T(8,128)(2,1)}, bf16[1,384,256]{2,1,0:T(8,128)(2,1)}, u32[]{:S(2)}, u32[]{:S(2)}) collective-permute-start(bf16[1,384,256]{2,1,0:T(8,128)(2,1)} %get-tuple-element.18), channel_id=1, source_target_pairs={{0,1},{1,2},{2,3},{3,4},{4,5},{5,6},{6,7},{7,8},{8,9},{9,10},{10,1... | collective-permute-start | bytes 589832 | tf_op jit(solution)/shard_map/ppermute | solution.py:14
  43.9 8.3 %collective-permute-start.3 = (bf16[1,384,256]{2,1,0:T(8,128)(2,1)}, bf16[1,384,256]{2,1,0:T(8,128)(2,1)S(1)}, u32[]{:S(2)}, u32[]{:S(2)}) collective-permute-start(bf16[1,384,256]{2,1,0:T(8,128)(2,1)} %get-tuple-element.19), channel_id=1, source_target_pairs={{1,0},{2,1},{3,2},{4,3},{5,4},{6,5},{7,6},{8,7},{9,8},{10,9},{11,1... | collective-permute-start | bytes 589832 | tf_op jit(solution)/shard_map/ppermute | solution.py:17
  46.9 7.7 %copy-start.2 = (bf16[2,384,256]{2,1,0:T(8,128)(2,1)S(1)}, bf16[2,384,256]{2,1,0:T(8,128)(2,1)}, u32[]{:S(2)}) copy-start(bf16[2,384,256]{2,1,0:T(8,128)(2,1)} %get-tuple-element.25) | copy-start | bytes 1179652
  53.3 1.6 %copy-start.8 = (bf16[2304,256]{1,0:T(8,128)(2,1)S(1)}, bf16[2304,256]{1,0:T(8,128)(2,1)}, u32[]{:S(2)}) copy-start(bf16[2304,256]{1,0:T(8,128)(2,1)} %param.26) | copy-start | bytes 3538948
  53.3 1.6 %copy-start.12 = (f32[256]{0:T(256)S(1)}, f32[256]{0:T(256)}, u32[]{:S(2)}) copy-start(f32[256]{0:T(256)} %param.27) | copy-start | bytes 3076
  54.9 5.7 %copy-start.5 = (bf16[256,256]{1,0:T(8,128)(2,1)S(1)}, bf16[256,256]{1,0:T(8,128)(2,1)}, u32[]{:S(2)}) copy-start(bf16[256,256]{1,0:T(8,128)(2,1)} %param.24) | copy-start | bytes 393220
  54.9 5.7 %copy-start.7 = (f32[256]{0:T(256)S(1)}, f32[256]{0:T(256)}, u32[]{:S(2)}) copy-start(f32[256]{0:T(256)} %param.25) | copy-start | bytes 3076
  56.1 4.8 %collective-permute-start.4 = (bf16[1,384,256]{2,1,0:T(8,128)(2,1)S(1)}, bf16[1,384,256]{2,1,0:T(8,128)(2,1)S(1)}, u32[]{:S(2)}, u32[]{:S(2)}) collective-permute-start(bf16[1,384,256]{2,1,0:T(8,128)(2,1)S(1)} %get-tuple-element.16), channel_id=1, source_target_pairs={{0,1},{1,2},{2,3},{3,4},{4,5},{5,6},{6,7},{7,8},{8,9},{9,10},{10,1... | collective-permute-start | bytes 589832 | tf_op jit(solution)/shard_map/ppermute | solution.py:14
  58.0 8.5 %collective-permute-start.5 = (bf16[1,384,256]{2,1,0:T(8,128)(2,1)S(1)}, bf16[1,384,256]{2,1,0:T(8,128)(2,1)S(1)}, u32[]{:S(2)}, u32[]{:S(2)}) collective-permute-start(bf16[1,384,256]{2,1,0:T(8,128)(2,1)S(1)} %get-tuple-element.17), channel_id=1, source_target_pairs={{1,0},{2,1},{3,2},{4,3},{5,4},{6,5},{7,6},{8,7},{9,8},{10,9},{11,1... | collective-permute-start | bytes 589832 | tf_op jit(solution)/shard_map/ppermute | solution.py:17
  69.2 4.5 %collective-permute-start.8 = (bf16[1,384,256]{2,1,0:T(8,128)(2,1)S(1)}, bf16[1,384,256]{2,1,0:T(8,128)(2,1)S(1)}, u32[]{:S(2)}, u32[]{:S(2)}) collective-permute-start(bf16[1,384,256]{2,1,0:T(8,128)(2,1)S(1)} %get-tuple-element.14), channel_id=1, source_target_pairs={{0,1},{1,2},{2,3},{3,4},{4,5},{5,6},{6,7},{7,8},{8,9},{9,10},{10,1... | collective-permute-start | bytes 589832 | tf_op jit(solution)/shard_map/ppermute | solution.py:14
  71.1 7.9 %collective-permute-start.9 = (bf16[1,384,256]{2,1,0:T(8,128)(2,1)S(1)}, bf16[1,384,256]{2,1,0:T(8,128)(2,1)S(1)}, u32[]{:S(2)}, u32[]{:S(2)}) collective-permute-start(bf16[1,384,256]{2,1,0:T(8,128)(2,1)S(1)} %get-tuple-element.15), channel_id=1, source_target_pairs={{1,0},{2,1},{3,2},{4,3},{5,4},{6,5},{7,6},{8,7},{9,8},{10,9},{11,1... | collective-permute-start | bytes 589832 | tf_op jit(solution)/shard_map/ppermute | solution.py:17
  79.2 1.3 %copy-start.10 = (bf16[2304,256]{1,0:T(8,128)(2,1)S(1)}, bf16[2304,256]{1,0:T(8,128)(2,1)}, u32[]{:S(2)}) copy-start(bf16[2304,256]{1,0:T(8,128)(2,1)} %param.30) | copy-start | bytes 3538948
  81.6 4.5 %collective-permute-start.10 = (bf16[1,384,256]{2,1,0:T(8,128)(2,1)S(1)}, bf16[1,384,256]{2,1,0:T(8,128)(2,1)S(1)}, u32[]{:S(2)}, u32[]{:S(2)}) collective-permute-start(bf16[1,384,256]{2,1,0:T(8,128)(2,1)S(1)} %get-tuple-element.12), channel_id=1, source_target_pairs={{0,1},{1,2},{2,3},{3,4},{4,5},{5,6},{6,7},{7,8},{8,9},{9,10},{10,1... | collective-permute-start | bytes 589832 | tf_op jit(solution)/shard_map/ppermute | solution.py:14
  83.5 7.9 %collective-permute-start.11 = (bf16[1,384,256]{2,1,0:T(8,128)(2,1)S(1)}, bf16[1,384,256]{2,1,0:T(8,128)(2,1)S(1)}, u32[]{:S(2)}, u32[]{:S(2)}) collective-permute-start(bf16[1,384,256]{2,1,0:T(8,128)(2,1)S(1)} %get-tuple-element.13), channel_id=1, source_target_pairs={{1,0},{2,1},{3,2},{4,3},{5,4},{6,5},{7,6},{8,7},{9,8},{10,9},{11,1... | collective-permute-start | bytes 589832 | tf_op jit(solution)/shard_map/ppermute | solution.py:17
  91.7 1.3 %copy-start.11 = (bf16[2304,256]{1,0:T(8,128)(2,1)S(1)}, bf16[2304,256]{1,0:T(8,128)(2,1)}, u32[]{:S(2)}) copy-start(bf16[2304,256]{1,0:T(8,128)(2,1)} %param.32) | copy-start | bytes 3538948
  (4 other events, 5.1 us)
where the time goes:
time: 96.6 us; the launch traced here: 94.8 us
  starting transfers between devices  30.4 us (31%)
  waiting for transfers between devices  22.1 us (23%)
  local copies, waits for them, and re-layouts  19.5 us (20%)
  matrix products  12.2 us (13%)
  other arithmetic  9.71 us (10%)
    ppermute x6, waiting for transfers between devices, padded(): lax.ppermute(lax.slice_in_dim(block, 0, width, axis=dim), axis, backward)  21.7 us
    ppermute x6, starting transfers between devices, padded(): lax.ppermute(lax.slice_in_dim(block, block.shape[dim] - width, None, axis...  16.6 us
    ppermute x6, starting transfers between devices, padded(): lax.ppermute(lax.slice_in_dim(block, 0, width, axis=dim), axis, backward)  13.8 us
    dot_general x5, matrix products, conv_block(): jnp.dot(columns.reshape(height * across, 9 * channels), weight, preferred...  7.82 us
    dot_general x1, matrix products, body(): jnp.dot(features.reshape(height * across, channels), lift_weight, preferr...  4.14 us
    unnamed x60, local copies, waits for them, and re-layouts  4.05 us
    slice x6, local copies, waits for them, and re-layouts, padded(): lax.slice_in_dim(block, block.shape[dim] - width, None, axis=dim)  4.04 us
    convert_element_type x2, local copies, waits for them, and re-layouts, body(): widened = lifted.transpose(0, 2, 1, 3, 4).reshape(2 * height, 2 * across,...  3.68 us
  transfers between devices with their start and end apart: 12, of which 7 were waited for; matrix products, arithmetic and copies ran while one was open for 24% of the time, Pallas kernels for 0%

commit v1 on v0

v1 whole, which is shorter than its diff:
```python
import functools

import jax
import jax.numpy as jnp
from jax import lax
from jax.experimental import pallas as pl
from jax.experimental.pallas import tpu as pltpu
from jax.sharding import PartitionSpec as P

GW = 192
QUAD = 4
SEG = GW // QUAD
HALO = 3
SENT = 56
SLOT = 64

BF16, F32 = jnp.bfloat16, jnp.float32
VMEM = pl.BlockSpec(memory_space=pltpu.VMEM)
ANY = pl.BlockSpec(memory_space=pl.ANY)


def place():
    position = lax.axis_index("rows")
    return lax.rem(position, QUAD), lax.div(position, QUAD)


def project_kernel(tap, coarse, weight, bias, *rest):
    segments, (grid, sparse) = rest[:QUAD], rest[QUAD:]
    own, _ = place()
    edge = grid.shape[0] - GW
    grid[0:8] = jnp.zeros((8, grid.shape[1]), F32)
    grid[GW:] = jnp.zeros((edge, grid.shape[1]), F32)
    grid[HALO : HALO + GW] = jnp.dot(tap[...], weight[...], preferred_element_type=F32) + bias[...]
    wide = coarse[...].astype(F32)
    sparse[0:8] = jnp.zeros((8, sparse.shape[1]), F32)
    sparse[GW:] = jnp.zeros((edge, sparse.shape[1]), F32)
    sparse[HALO : HALO + GW] = wide
    sparse[HALO - 1 : HALO] = wide[:1]
    sparse[HALO + GW : HALO + GW + 1] = wide[GW - 1 :]
    split = grid.shape[1]
    for k in range(QUAD):
        start = pl.multiple_of(lax.bitwise_xor(own, k) * SEG, 16)
        segments[k][:, :split] = grid[pl.ds(start, SENT), :].astype(BF16)
        segments[k][:, split:] = sparse[pl.ds(start, SENT), :].astype(BF16)


def pack_kernel(split, *refs):
    segments, (block, first, second) = refs[:QUAD], refs[QUAD:]
    own, number = place()
    for row in range(QUAD):
        for k in range(QUAD):

            @pl.when(own == row ^ k)
            def _():
                block[row * SENT : (row + 1) * SENT] = segments[k][...]

    coarse = block.shape[1] - split
    even = lax.rem(number, 2) == 0

    def fill(payload, row, coarse_row):
        payload[: HALO * SENT] = block[row * SENT : (row + HALO) * SENT, :split]
        for half in range(2):
            payload[HALO * SENT :, half * coarse : (half + 1) * coarse] = block[
                (coarse_row + half) * SENT : (coarse_row + half + 1) * SENT, split:
            ]

    @pl.when(even)
    def _():
        fill(first, 1, 2)
        fill(second, 0, 0)

    @pl.when(jnp.logical_not(even))
    def _():
        fill(first, 0, 0)
        fill(second, 1, 2)


def spread_out(target, row, rows, width, even, odd):
    count = rows * SLOT
    here = slice(row * SLOT, row * SLOT + count)
    target[here, :width] = pltpu.roll(odd, 1, 0).astype(BF16)
    target[here, width : 2 * width] = even.astype(BF16)
    target[here, 2 * width : 3 * width] = odd.astype(BF16)
    target[here, 3 * width :] = pltpu.roll(even, count - 1, 0).astype(BF16)


def unite_kernel(blocks, *refs):
    (block, first, second, lift_w, lift_b, merge_w, out_w, out_b) = refs[:8]
    (inner1_w, inner1_b, outer1_w, outer1_b, inner2_w, inner2_b, outer2_w, outer2_b) = refs[8:16]
    outs = refs[16 : 16 + QUAD]
    (lift_v, out_v, merge_v, inner1_v, outer1_v, inner2_v, outer2_v) = refs[20:27]
    (window, coarse, thin, mask, wide_x, x_a, x_b, kept_r, kept_m, fine) = refs[27:37]
    sems = refs[37]
    own, number = place()
    split = window.shape[1]
    width = x_a.shape[1] // 4

    copies = [
        pltpu.make_async_copy(source, target, sems.at[i])
        for i, (source, target) in enumerate(
            (
                (lift_w, lift_v),
                (merge_w, merge_v),
                (out_w, out_v),
                (inner1_w, inner1_v),
                (outer1_w, outer1_v),
                (inner2_w, inner2_v),
                (outer2_w, outer2_v),
            )
        )
    ]
    for copy in copies:
        copy.start()

    rows_w = mask.shape[0] // SLOT
    lane = lax.broadcasted_iota(jnp.int32, (SLOT, 128), 0)
    token = lane + (own * SEG - HALO)
    inside = (token >= 0) & (token < GW) & (lane < SEG + 2 * HALO)
    inside = jnp.where(inside, 1.0, 0.0)
    for r in range(rows_w):
        at = number * (2 * QUAD) + (r - 5)
        good = jnp.where((at >= 0) & (at < blocks * 2 * QUAD), 1.0, 0.0)
        mask[r * SLOT : (r + 1) * SLOT] = inside * good

    def masked(value, row, rows):
        keep = mask[row * SLOT : (row + rows) * SLOT]
        keep = jnp.concatenate([keep] * (value.shape[1] // 128), axis=1)
        return jnp.where(keep > 0.5, value, 0.0)

    tail = SLOT - SENT
    for i in range(QUAD + 2 * HALO):
        window[i * SLOT + SENT : (i + 1) * SLOT] = jnp.zeros((tail, split), BF16)
    for i in range(QUAD + 4):
        coarse[i * SLOT + SENT : (i + 1) * SLOT] = jnp.zeros((tail, width), BF16)
    for i in range(QUAD):
        there = slice(i * SENT, (i + 1) * SENT)
        at = (i + HALO) * SLOT
        window[at : at + SENT] = block[there, :split]
        at = (i + 2) * SLOT
        coarse[at : at + SENT] = block[there, split:]

    def land(payload, row, coarse_row):
        for i in range(HALO):
            at = (row + i) * SLOT
            window[at : at + SENT] = payload[i * SENT : (i + 1) * SENT]
        for half in range(2):
            at = (coarse_row + half) * SLOT
            coarse[at : at + SENT] = payload[HALO * SENT :, half * width : (half + 1) * width]

    even_block = lax.rem(number, 2) == 0

    @pl.when(even_block)
    def _():
        land(second, 0, 0)
        land(first, QUAD + HALO, QUAD + 2)

    @pl.when(jnp.logical_not(even_block))
    def _():
        land(first, 0, 0)
        land(second, QUAD + HALO, QUAD + 2)

    @pl.when(number == 0)
    def _():
        coarse[SLOT : SLOT + SENT] = block[:SENT, split:]

    @pl.when(number == blocks - 1)
    def _():
        at = (QUAD + 2) * SLOT
        coarse[at : at + SENT] = block[(QUAD - 1) * SENT :, split:]

    copies[0].wait()
    tall = rows_w // 2
    for a in range(2):
        lhs = window[(1 - a) * SLOT : (1 - a + tall) * SLOT]
        for b in range(2):
            lifted = jnp.dot(
                lhs,
                lift_v[:, (2 * a + b) * split : (2 * a + b + 1) * split],
                preferred_element_type=F32,
            )
            for i in range(tall):
                row = 2 * i + (1 - a)
                value = masked(lifted[i * SLOT : (i + 1) * SLOT] + lift_b[...], row, 1)
                here = slice(row * SLOT, (row + 1) * SLOT)
                plain, moved = (1, 3) if b == 0 else (2, 0)
                shift = SLOT - 1 if b == 0 else 1
                wide_x[here, plain * split : (plain + 1) * split] = value.astype(BF16)
                wide_x[here, moved * split : (moved + 1) * split] = pltpu.roll(
                    value, shift, 0
                ).astype(BF16)

    def conv(source, weight, channels, row, rows):
        total = None
        for dy in range(3):
            piece = source[(row + dy) * SLOT : (row + dy + rows) * SLOT]
            lhs = jnp.concatenate([piece[:, : 3 * channels], piece[:, channels:]], axis=0)
            part = jnp.dot(
                lhs,
                weight[3 * dy * channels : 3 * (dy + 1) * channels],
                preferred_element_type=F32,
            )
            total = part if total is None else total + part
        return total[: rows * SLOT], total[rows * SLOT :]

    def chunks(rows, size):
        return [(row, min(size, rows - row)) for row in range(0, rows, size)]

    copies[1].wait()
    for row, rows in chunks(rows_w - 2, 4):
        even, odd = conv(wide_x, merge_v, split, row, rows)
        here = slice(row * SLOT, (row + rows) * SLOT)
        kept_r[0, here] = even.astype(BF16)
        kept_r[1, here] = odd.astype(BF16)
        even = masked(jnp.maximum(even, 0.0), row + 1, rows)
        odd = masked(jnp.maximum(odd, 0.0), row + 1, rows)
        spread_out(x_a, row, rows, width, even, odd)

    copies[2].wait()
    thin[...] = jnp.dot(coarse[...], out_v[...], preferred_element_type=F32)

    copies[3].wait()
    for row, rows in chunks(rows_w - 4, 7):
        even, odd = conv(x_a, inner1_v, width, row, rows)
        even = masked(jnp.maximum(even + inner1_b[...], 0.0), row + 2, rows)
        odd = masked(jnp.maximum(odd + inner1_b[...], 0.0), row + 2, rows)
        spread_out(x_b, row, rows, width, even, odd)

    copies[4].wait()
    bias = outer1_b[...] + out_b[...]
    for row, rows in chunks(rows_w - 6, 4):
        even, odd = conv(x_b, outer1_v, width, row, rows)
        left, right = [], []
        for r in range(row, row + rows):
            i, a = divmod(r + 2, 2)
            near = thin[i * SLOT : (i + 1) * SLOT]
            far = i - 1 if a == 0 else i + 1
            band = 0.75 * near + 0.25 * thin[far * SLOT : (far + 1) * SLOT]
            left.append(0.25 * pltpu.roll(band, 1, 0) + 0.75 * band)
            right.append(0.75 * band + 0.25 * pltpu.roll(band, SLOT - 1, 0))
        old = slice((row + 2) * SLOT, (row + 2 + rows) * SLOT)
        even = even + bias + kept_r[0, old].astype(F32) + jnp.concatenate(left, axis=0)
        odd = odd + bias + kept_r[1, old].astype(F32) + jnp.concatenate(right, axis=0)
        here = slice(row * SLOT, (row + rows) * SLOT)
        kept_m[0, here] = even.astype(BF16)
        kept_m[1, here] = odd.astype(BF16)
        even = masked(jnp.maximum(even, 0.0), row + 3, rows)
        odd = masked(jnp.maximum(odd, 0.0), row + 3, rows)
        spread_out(x_a, row, rows, width, even, odd)

    copies[5].wait()
    for row, rows in chunks(rows_w - 8, 5):
        even, odd = conv(x_a, inner2_v, width, row, rows)
        even = masked(jnp.maximum(even + inner2_b[...], 0.0), row + 4, rows)
        odd = masked(jnp.maximum(odd + inner2_b[...], 0.0), row + 4, rows)
        spread_out(x_b, row, rows, width, even, odd)

    copies[6].wait()
    for row, rows in chunks(rows_w - 10, 4):
        pair = conv(x_b, outer2_v, width, row, rows)
        for parity in range(2):
            old = slice((row + 2) * SLOT, (row + 2 + rows) * SLOT)
            value = pair[parity] + outer2_b[...] + kept_m[parity, old].astype(F32)
            for r in range(rows):
                cells = value[r * SLOT + HALO : r * SLOT + HALO + SEG]
                base = (row + r) * 2 * SEG + parity
                for half in range(width // 128):
                    fine[half, pl.ds(base, SEG, 2), :] = cells[:, half * 128 : (half + 1) * 128]
    for k in range(QUAD):
        start = pl.multiple_of(lax.bitwise_xor(own, k) * (4 * SEG), 16)
        for half in range(width // 128):
            outs[k][:, half * 128 : (half + 1) * 128] = fine[half, pl.ds(start, 4 * SEG), :].astype(
                BF16
            )


def assemble_kernel(*refs):
    pieces, out = refs[:QUAD], refs[QUAD]
    own, _ = place()
    for k in range(QUAD):
        start = pl.multiple_of(lax.bitwise_xor(own, k) * (2 * SEG), 16)
        for r in range(2):
            out[r, pl.ds(start, 2 * SEG), :] = pieces[k][r * 2 * SEG : (r + 1) * 2 * SEG]


def body(
    tap_two,
    coarse_path,
    proj_weight,
    proj_bias,
    lift_weight,
    lift_bias,
    merge_weight,
    out_weight,
    out_bias,
    first_inner_w,
    first_inner_b,
    first_outer_w,
    first_outer_b,
    second_inner_w,
    second_inner_b,
    second_outer_w,
    second_outer_b,
):
    count = lax.axis_size("rows")
    if tap_two.shape[0] != GW or count % QUAD:
        raise ValueError("unsupported split")
    blocks = count // QUAD
    split = proj_weight.shape[1]
    width = out_weight.shape[1]
    shape = jax.ShapeDtypeStruct

    def swap(value, k):
        return lax.ppermute(value, "rows", [(i, i ^ k) for i in range(count)])

    def between(value, parity):
        pairs = []
        for low in range(parity, blocks - 1, 2):
            for q in range(QUAD):
                a, b = low * QUAD + q, (low + 1) * QUAD + q
                pairs += [(a, b), (b, a)]
        return lax.ppermute(value, "rows", pairs)

    segments = pl.pallas_call(
        project_kernel,
        out_shape=[shape((SENT, split + width), BF16)] * QUAD,
        in_specs=[VMEM] * 4,
        out_specs=[VMEM] * QUAD,
        scratch_shapes=[pltpu.VMEM((GW + 16, split), F32), pltpu.VMEM((GW + 16, width), F32)],
    )(tap_two, coarse_path, proj_weight, proj_bias[None])
    segments = [segments[0]] + [swap(segments[k], k) for k in range(1, QUAD)]
    block, first, second = pl.pallas_call(
        functools.partial(pack_kernel, split),
        out_shape=[shape((QUAD * SENT, split + width), BF16)]
        + [shape(((HALO + 1) * SENT, split), BF16)] * 2,
        in_specs=[VMEM] * QUAD,
        out_specs=[VMEM] * 3,
    )(*segments)
    first, second = between(first, 0), between(second, 1)

    rows_w = 2 * QUAD + 10
    weights = (
        lift_weight,
        out_weight,
        merge_weight,
        first_inner_w,
        first_outer_w,
        second_inner_w,
        second_outer_w,
    )
    flops = 2 * rows_w * SLOT * (2 * split * split + 4 * 9 * split * width)
    outs = pl.pallas_call(
        functools.partial(unite_kernel, blocks),
        out_shape=[shape((4 * SEG, width), BF16)] * QUAD,
        in_specs=[VMEM] * 3
        + [ANY, VMEM, ANY, ANY, VMEM, ANY, VMEM, ANY, VMEM, ANY, VMEM, ANY, VMEM],
        out_specs=[VMEM] * QUAD,
        scratch_shapes=[pltpu.VMEM(w.shape, BF16) for w in weights]
        + [
            pltpu.VMEM(((QUAD + 2 * HALO) * SLOT, split), BF16),
            pltpu.VMEM(((QUAD + 4) * SLOT, width), BF16),
            pltpu.VMEM(((QUAD + 4) * SLOT, width), F32),
            pltpu.VMEM((rows_w * SLOT, 128), F32),
            pltpu.VMEM((rows_w * SLOT, 4 * split), BF16),
            pltpu.VMEM(((rows_w - 2) * SLOT, 4 * width), BF16),
            pltpu.VMEM(((rows_w - 4) * SLOT, 4 * width), BF16),
            pltpu.VMEM((2, (rows_w - 2) * SLOT, width), BF16),
            pltpu.VMEM((2, (rows_w - 6) * SLOT, width), BF16),
            pltpu.VMEM((width // 128, 4 * QUAD * SEG, 128), F32),
            pltpu.SemaphoreType.DMA((7,)),
        ],
        compiler_params=pltpu.CompilerParams(vmem_limit_bytes=60 * 1024 * 1024),
        cost_estimate=pl.CostEstimate(flops=flops, bytes_accessed=10_000_000, transcendentals=0),
    )(
        block,
        first,
        second,
        lift_weight,
        lift_bias[None],
        merge_weight,
        out_weight,
        out_bias[None],
        first_inner_w,
        first_inner_b[None],
        first_outer_w,
        first_outer_b[None],
        second_inner_w,
        second_inner_b[None],
        second_outer_w,
        second_outer_b[None],
    )
    pieces = [outs[0]] + [swap(outs[k], k) for k in range(1, QUAD)]
    return pl.pallas_call(
        assemble_kernel,
        out_shape=shape((2, 2 * GW, width), BF16),
        in_specs=[VMEM] * QUAD,
        out_specs=VMEM,
    )(*pieces)


def solution(mesh):
    return jax.shard_map(
        body,
        mesh=mesh,
        in_specs=(P(("groups", "rows"), None), P(("groups", "rows"), None)) + (P(),) * 15,
        out_specs=P(("groups", "rows"), None, None),
        check_vma=False,
    )
```

time: 96.6 us -> 53.7 us (0.56); the launches traced: 94.8 us -> 53.2 us
  Pallas kernels: 0 us -> 26.1 us
  starting transfers between devices: 30.4 us -> 9.69 us
  local copies, waits for them, and re-layouts: 19.5 us -> 1.98 us
  matrix products: 12.2 us -> 0 us
  other arithmetic: 9.71 us -> 0 us
  waiting for transfers between devices: 22.1 us -> 15.4 us
    pallas_call x0 -> x4, Pallas kernels: none -> 26.1 us  [the longest x1 19.8 us: body(): pl.pallas_call(functools.partial(unite_kernel, blocks), out_shape=[shape(...]
    ppermute x12 -> x8, starting transfers between devices: 30.4 us -> 9.69 us  [the longest x6 5.21 us: swap(): return lax.ppermute(value, 'rows', [(i, i ^ k) for i in range(count)])]
    dot_general x7 -> x0, matrix products: 12.2 us -> none  [the longest x5 7.82 us: conv_block(): jnp.dot(columns.reshape(height * across, 9 * channels), weight, preferred...]
    ppermute x12 -> x8, waiting for transfers between devices: 22.1 us -> 15.4 us  [the longest x6 9.79 us: swap(): return lax.ppermute(value, 'rows', [(i, i ^ k) for i in range(count)])]
    slice x8 -> x0, local copies, waits for them, and re-layouts: 4.98 us -> none  [the longest x6 4.04 us: padded(): lax.slice_in_dim(block, block.shape[dim] - width, None, axis=dim)]
    convert_element_type x2 -> x0, local copies, waits for them, and re-layouts: 3.68 us -> none  [body(): widened = lifted.transpose(0, 2, 1, 3, 4).reshape(2 * height, 2 * across,...]
    reshape x1 -> x0, local copies, waits for them, and re-layouts: 3.41 us -> none  [body(): lifted = lifted.reshape(height, across, 2, 2, channels) + lift_bias]
    concatenate x7 -> x0, other arithmetic: 3.2 us -> none  [the longest x5 3.09 us: padded(): block = jnp.concatenate([low, block, high], axis=dim)]
  transfers between devices with their start and end apart: 12 -> 8, of which waited for: 7 -> 6; matrix products, arithmetic and copies ran while one was open for 24% -> 0% of each run, Pallas kernels for 0% -> 0%
where the time goes in v1:
time: 53.7 us; the launch traced here: 53.2 us
  Pallas kernels  26.1 us (49%)
  waiting for transfers between devices  15.4 us (29%)
  starting transfers between devices  9.69 us (18%)
  local copies, waits for them, and re-layouts  1.98 us (4%)
    pallas_call x1, Pallas kernels, body(): pl.pallas_call(functools.partial(unite_kernel, blocks), out_shape=[shape(...  19.8 us
    ppermute x6, waiting for transfers between devices, swap(): return lax.ppermute(value, 'rows', [(i, i ^ k) for i in range(count)])  9.79 us
    ppermute x2, waiting for transfers between devices, between(): return lax.ppermute(value, 'rows', pairs)  5.64 us
    ppermute x6, starting transfers between devices, swap(): return lax.ppermute(value, 'rows', [(i, i ^ k) for i in range(count)])  5.21 us
    ppermute x2, starting transfers between devices, between(): return lax.ppermute(value, 'rows', pairs)  4.49 us
    pallas_call x1, Pallas kernels, body(): pl.pallas_call(project_kernel, out_shape=[shape((SENT, split + width), BF...  2.54 us
    pallas_call x1, Pallas kernels, body(): pl.pallas_call(functools.partial(pack_kernel, split), out_shape=[shape((Q...  1.98 us
    unnamed x16, local copies, waits for them, and re-layouts  1.98 us
  transfers between devices with their start and end apart: 8, of which 6 were waited for; matrix products, arithmetic and copies ran while one was open for 0% of the time, Pallas kernels for 0%

profile of v1, /device:TPU:9, one launch (start us, length us, event | category | flops | bytes accessed | tf_op | source)
XLA Modules:
  0.0 53.2 jit_solution(14694191421927949462)
XLA Ops:
  0.0 2.5 %shard_map.163 = (bf16[56,768]{1,0:T(8,128)(2,1)}, bf16[56,768]{1,0:T(8,128)(2,1)}, bf16[56,768]{1,0:T(8,128)(2,1)}, bf16[56,768]{1,0:T(8,128)(2,1)}) custom-call(bf16[192,1024]{1,0:T(8,128)(2,1)} %tap.1, bf16[192,256]{1,0:T(8,128)(2,1)} %coarse.1, bf16[1024,512]{1,0:T(8,128)(2,1)} %weight.1, f32[1,512]{1,0:T(1,128)} %bitcast.7), custom_call_target="tpu_custom_call" | custom-call | tf_op jit(solution)/shard_map/pallas_call | solution.py:323
  2.5 0.7 %collective-permute-start = (bf16[56,768]{1,0:T(8,128)(2,1)}, bf16[56,768]{1,0:T(8,128)(2,1)S(1)}, u32[]{:S(2)}, u32[]{:S(2)}) collective-permute-start(bf16[56,768]{1,0:T(8,128)(2,1)} %get-tuple-element.17), channel_id=1, source_target_pairs={{0,1},{1,0},{2,3},{3,2},{4,5},{5,4},{6,7},{7,6},{8,9},{9,8},{10,11... | collective-permute-start | bytes 258056 | tf_op jit(solution)/shard_map/ppermute | solution.py:313
  3.2 1.2 %collective-permute-start.1 = (bf16[56,768]{1,0:T(8,128)(2,1)}, bf16[56,768]{1,0:T(8,128)(2,1)S(1)}, u32[]{:S(2)}, u32[]{:S(2)}) collective-permute-start(bf16[56,768]{1,0:T(8,128)(2,1)} %get-tuple-element.18), channel_id=1, source_target_pairs={{0,2},{1,3},{2,0},{3,1},{4,6},{5,7},{6,4},{7,5},{8,10},{9,11},{10,... | collective-permute-start | bytes 258056 | tf_op jit(solution)/shard_map/ppermute | solution.py:313
  4.5 0.4 collective-permute-start.2
  4.9 0.0 collective-permute-done.refs_1_
  4.9 2.6 %collective-permute-done.1.refs_2_ = bf16[56,768]{1,0:T(8,128)(2,1)S(1)} collective-permute-done((bf16[56,768]{1,0:T(8,128)(2,1)}, bf16[56,768]{1,0:T(8,128)(2,1)S(1)}, u32[]{:S(2)}, u32[]{:S(2)}) %collective-permute-start.1) | collective-permute-done | bytes 86048 | tf_op jit(solution)/shard_map/ppermute | solution.py:313
  7.5 2.0 %collective-permute-done.2.refs_3_ = bf16[56,768]{1,0:T(8,128)(2,1)S(1)} collective-permute-done((bf16[56,768]{1,0:T(8,128)(2,1)}, bf16[56,768]{1,0:T(8,128)(2,1)S(1)}, u32[]{:S(2)}, u32[]{:S(2)}) %collective-permute-start.2) | collective-permute-done | bytes 86048 | tf_op jit(solution)/shard_map/ppermute | solution.py:313
  9.5 0.0 copy-done.4
  9.5 0.6 %copy-done.5 = bf16[56,768]{1,0:T(8,128)(2,1)} copy-done((bf16[56,768]{1,0:T(8,128)(2,1)}, bf16[56,768]{1,0:T(8,128)(2,1)S(1)}, u32[]{:S(2)}) %copy-start.5) | copy-done | bytes 86040
  10.2 2.0 %shard_map.164 = (bf16[224,768]{1,0:T(8,128)(2,1)}, bf16[224,512]{1,0:T(8,128)(2,1)}, bf16[224,512]{1,0:T(8,128)(2,1)}) custom-call(bf16[56,768]{1,0:T(8,128)(2,1)} %get-tuple-element.16.refs_0_, bf16[56,768]{1,0:T(8,128)(2,1)} %copy-done.3, bf16[56,768]{1,0:T(8,128)(2,1)} %copy-done.4, bf16[56,768]{1,0:T(8,128)(2,1)} %copy-done.5), custom_call_target="tpu_custom_call" | custom-call | tf_op jit(solution)/shard_map/pallas_call | solution.py:331
  12.1 0.0 collective-permute-start.3
  12.2 4.4 %collective-permute-start.4 = (bf16[224,512]{1,0:T(8,128)(2,1)}, bf16[224,512]{1,0:T(8,128)(2,1)S(1)}, u32[]{:S(2)}, u32[]{:S(2)}) collective-permute-start(bf16[224,512]{1,0:T(8,128)(2,1)} %get-tuple-element.22), channel_id=1, source_target_pairs={{4,8},{8,4},{5,9},{9,5},{6,10},{10,6},{7,11},{11,7},{20,24},{24,20... | collective-permute-start | bytes 688136 | tf_op jit(solution)/shard_map/ppermute | solution.py:321
  16.6 2.6 %collective-permute-done.3.refs_1_ = bf16[224,512]{1,0:T(8,128)(2,1)S(1)} collective-permute-done((bf16[224,512]{1,0:T(8,128)(2,1)}, bf16[224,512]{1,0:T(8,128)(2,1)S(1)}, u32[]{:S(2)}, u32[]{:S(2)}) %collective-permute-start.3) | collective-permute-done | bytes 229408 | tf_op jit(solution)/shard_map/ppermute | solution.py:321
  19.3 3.0 %collective-permute-done.4.refs_2_ = bf16[224,512]{1,0:T(8,128)(2,1)S(1)} collective-permute-done((bf16[224,512]{1,0:T(8,128)(2,1)}, bf16[224,512]{1,0:T(8,128)(2,1)S(1)}, u32[]{:S(2)}, u32[]{:S(2)}) %collective-permute-start.4) | collective-permute-done | bytes 229408 | tf_op jit(solution)/shard_map/ppermute | solution.py:321
  22.3 0.7 %copy-done.7 = bf16[224,512]{1,0:T(8,128)(2,1)} copy-done((bf16[224,512]{1,0:T(8,128)(2,1)}, bf16[224,512]{1,0:T(8,128)(2,1)S(1)}, u32[]{:S(2)}) %copy-start.7) | copy-done | bytes 229400
  23.0 19.8 %shard_map.165 = (bf16[192,256]{1,0:T(8,128)(2,1)}, bf16[192,256]{1,0:T(8,128)(2,1)}, bf16[192,256]{1,0:T(8,128)(2,1)}, bf16[192,256]{1,0:T(8,128)(2,1)}) custom-call(bf16[224,768]{1,0:T(8,128)(2,1)} %get-tuple-element.20.refs_0_, bf16[224,512]{1,0:T(8,128)(2,1)} %copy-done.6, bf16[224,512]{1,0:T(8,128)(2,1)} %copy-done.7, bf16[512,2048]{1,0:T(8,128)(2,1)} %refs_3_.1, ...), custom_call_target="tpu_custom_call" | custom-call | flops 12079595520 | bytes 10000000 | tf_op jit(solution)/shard_map/pallas_call | solution.py:351
  42.8 1.2 %collective-permute-start.5 = (bf16[192,256]{1,0:T(8,128)(2,1)}, bf16[192,256]{1,0:T(8,128)(2,1)S(1)}, u32[]{:S(2)}, u32[]{:S(2)}) collective-permute-start(bf16[192,256]{1,0:T(8,128)(2,1)} %get-tuple-element.24), channel_id=1, source_target_pairs={{0,1},{1,0},{2,3},{3,2},{4,5},{5,4},{6,7},{7,6},{8,9},{9,8},{10,11... | collective-permute-start | bytes 294920 | tf_op jit(solution)/shard_map/ppermute | solution.py:313
  43.9 1.3 %collective-permute-start.6 = (bf16[192,256]{1,0:T(8,128)(2,1)}, bf16[192,256]{1,0:T(8,128)(2,1)S(1)}, u32[]{:S(2)}, u32[]{:S(2)}) collective-permute-start(bf16[192,256]{1,0:T(8,128)(2,1)} %get-tuple-element.25), channel_id=1, source_target_pairs={{0,2},{1,3},{2,0},{3,1},{4,6},{5,7},{6,4},{7,5},{8,10},{9,11},{10,... | collective-permute-start | bytes 294920 | tf_op jit(solution)/shard_map/ppermute | solution.py:313
  45.2 0.5 collective-permute-start.7
  45.6 0.0 collective-permute-done.5.refs_1_
  45.6 2.8 %collective-permute-done.6.refs_2_ = bf16[192,256]{1,0:T(8,128)(2,1)S(1)} collective-permute-done((bf16[192,256]{1,0:T(8,128)(2,1)}, bf16[192,256]{1,0:T(8,128)(2,1)S(1)}, u32[]{:S(2)}, u32[]{:S(2)}) %collective-permute-start.6) | collective-permute-done | bytes 98336 | tf_op jit(solution)/shard_map/ppermute | solution.py:313
  48.4 2.4 %collective-permute-done.7.refs_3_ = bf16[192,256]{1,0:T(8,128)(2,1)S(1)} collective-permute-done((bf16[192,256]{1,0:T(8,128)(2,1)}, bf16[192,256]{1,0:T(8,128)(2,1)S(1)}, u32[]{:S(2)}, u32[]{:S(2)}) %collective-permute-start.7) | collective-permute-done | bytes 98336 | tf_op jit(solution)/shard_map/ppermute | solution.py:313
  50.8 0.6 %copy-done.2 = bf16[192,256]{1,0:T(8,128)(2,1)} copy-done((bf16[192,256]{1,0:T(8,128)(2,1)}, bf16[192,256]{1,0:T(8,128)(2,1)S(1)}, u32[]{:S(2)}) %copy-start.2) | copy-done | bytes 98328
  51.4 1.8 %shard_map.166 = bf16[2,384,256]{2,1,0:T(8,128)(2,1)} custom-call(bf16[192,256]{1,0:T(8,128)(2,1)} %get-tuple-element.23.refs_0_, bf16[192,256]{1,0:T(8,128)(2,1)} %copy-done, bf16[192,256]{1,0:T(8,128)(2,1)} %copy-done.1, bf16[192,256]{1,0:T(8,128)(2,1)} %copy-done.2), custom_call_target="tpu_custom_call" | custom-call | tf_op jit(solution)/shard_map/pallas_call | solution.py:392
  (12 shorter events, 0.0 us)
Async XLA Ops:
  2.5 2.3 %collective-permute-start = (bf16[56,768]{1,0:T(8,128)(2,1)}, bf16[56,768]{1,0:T(8,128)(2,1)S(1)}, u32[]{:S(2)}, u32[]{:S(2)}) collective-permute-start(bf16[56,768]{1,0:T(8,128)(2,1)} %get-tuple-element.17), channel_id=1, source_target_pairs={{0,1},{1,0},{2,3},{3,2},{4,5},{5,4},{6,7},{7,6},{8,9},{9,8},{10,11... | collective-permute-start | bytes 258056 | tf_op jit(solution)/shard_map/ppermute | solution.py:313
  3.2 4.3 %collective-permute-start.1 = (bf16[56,768]{1,0:T(8,128)(2,1)}, bf16[56,768]{1,0:T(8,128)(2,1)S(1)}, u32[]{:S(2)}, u32[]{:S(2)}) collective-permute-start(bf16[56,768]{1,0:T(8,128)(2,1)} %get-tuple-element.18), channel_id=1, source_target_pairs={{0,2},{1,3},{2,0},{3,1},{4,6},{5,7},{6,4},{7,5},{8,10},{9,11},{10,... | collective-permute-start | bytes 258056 | tf_op jit(solution)/shard_map/ppermute | solution.py:313
  4.5 5.1 %collective-permute-start.2 = (bf16[56,768]{1,0:T(8,128)(2,1)}, bf16[56,768]{1,0:T(8,128)(2,1)S(1)}, u32[]{:S(2)}, u32[]{:S(2)}) collective-permute-start(bf16[56,768]{1,0:T(8,128)(2,1)} %get-tuple-element.19), channel_id=1, source_target_pairs={{0,3},{1,2},{2,1},{3,0},{4,7},{5,6},{6,5},{7,4},{8,11},{9,10},{10,... | collective-permute-start | bytes 258056 | tf_op jit(solution)/shard_map/ppermute | solution.py:313
  4.9 4.7 %copy-start.3 = (bf16[56,768]{1,0:T(8,128)(2,1)}, bf16[56,768]{1,0:T(8,128)(2,1)S(1)}, u32[]{:S(2)}) copy-start(bf16[56,768]{1,0:T(8,128)(2,1)S(1)} %collective-permute-done.refs_1_) | copy-start | bytes 258052
  7.5 2.0 %copy-start.4 = (bf16[56,768]{1,0:T(8,128)(2,1)}, bf16[56,768]{1,0:T(8,128)(2,1)S(1)}, u32[]{:S(2)}) copy-start(bf16[56,768]{1,0:T(8,128)(2,1)S(1)} %collective-permute-done.1.refs_2_) | copy-start | bytes 258052
  9.5 0.6 %copy-start.5 = (bf16[56,768]{1,0:T(8,128)(2,1)}, bf16[56,768]{1,0:T(8,128)(2,1)S(1)}, u32[]{:S(2)}) copy-start(bf16[56,768]{1,0:T(8,128)(2,1)S(1)} %collective-permute-done.2.refs_3_) | copy-start | bytes 258052
  12.1 7.1 %collective-permute-start.3 = (bf16[224,512]{1,0:T(8,128)(2,1)}, bf16[224,512]{1,0:T(8,128)(2,1)S(1)}, u32[]{:S(2)}, u32[]{:S(2)}) collective-permute-start(bf16[224,512]{1,0:T(8,128)(2,1)} %get-tuple-element.21), channel_id=1, source_target_pairs={{0,4},{4,0},{1,5},{5,1},{2,6},{6,2},{3,7},{7,3},{8,12},{12,8},{9,1... | collective-permute-start | bytes 688136 | tf_op jit(solution)/shard_map/ppermute | solution.py:321
  12.2 10.1 %collective-permute-start.4 = (bf16[224,512]{1,0:T(8,128)(2,1)}, bf16[224,512]{1,0:T(8,128)(2,1)S(1)}, u32[]{:S(2)}, u32[]{:S(2)}) collective-permute-start(bf16[224,512]{1,0:T(8,128)(2,1)} %get-tuple-element.22), channel_id=1, source_target_pairs={{4,8},{8,4},{5,9},{9,5},{6,10},{10,6},{7,11},{11,7},{20,24},{24,20... | collective-permute-start | bytes 688136 | tf_op jit(solution)/shard_map/ppermute | solution.py:321
  19.3 3.0 %copy-start.6 = (bf16[224,512]{1,0:T(8,128)(2,1)}, bf16[224,512]{1,0:T(8,128)(2,1)S(1)}, u32[]{:S(2)}) copy-start(bf16[224,512]{1,0:T(8,128)(2,1)S(1)} %collective-permute-done.3.refs_1_) | copy-start | bytes 688132
  22.3 0.7 %copy-start.7 = (bf16[224,512]{1,0:T(8,128)(2,1)}, bf16[224,512]{1,0:T(8,128)(2,1)S(1)}, u32[]{:S(2)}) copy-start(bf16[224,512]{1,0:T(8,128)(2,1)S(1)} %collective-permute-done.4.refs_2_) | copy-start | bytes 688132
  42.8 2.9 %collective-permute-start.5 = (bf16[192,256]{1,0:T(8,128)(2,1)}, bf16[192,256]{1,0:T(8,128)(2,1)S(1)}, u32[]{:S(2)}, u32[]{:S(2)}) collective-permute-start(bf16[192,256]{1,0:T(8,128)(2,1)} %get-tuple-element.24), channel_id=1, source_target_pairs={{0,1},{1,0},{2,3},{3,2},{4,5},{5,4},{6,7},{7,6},{8,9},{9,8},{10,11... | collective-permute-start | bytes 294920 | tf_op jit(solution)/shard_map/ppermute | solution.py:313
  43.9 4.5 %collective-permute-start.6 = (bf16[192,256]{1,0:T(8,128)(2,1)}, bf16[192,256]{1,0:T(8,128)(2,1)S(1)}, u32[]{:S(2)}, u32[]{:S(2)}) collective-permute-start(bf16[192,256]{1,0:T(8,128)(2,1)} %get-tuple-element.25), channel_id=1, source_target_pairs={{0,2},{1,3},{2,0},{3,1},{4,6},{5,7},{6,4},{7,5},{8,10},{9,11},{10,... | collective-permute-start | bytes 294920 | tf_op jit(solution)/shard_map/ppermute | solution.py:313
  45.2 5.6 %collective-permute-start.7 = (bf16[192,256]{1,0:T(8,128)(2,1)}, bf16[192,256]{1,0:T(8,128)(2,1)S(1)}, u32[]{:S(2)}, u32[]{:S(2)}) collective-permute-start(bf16[192,256]{1,0:T(8,128)(2,1)} %get-tuple-element.26), channel_id=1, source_target_pairs={{0,3},{1,2},{2,1},{3,0},{4,7},{5,6},{6,5},{7,4},{8,11},{9,10},{10,... | collective-permute-start | bytes 294920 | tf_op jit(solution)/shard_map/ppermute | solution.py:313
  45.6 5.1 %copy-start = (bf16[192,256]{1,0:T(8,128)(2,1)}, bf16[192,256]{1,0:T(8,128)(2,1)S(1)}, u32[]{:S(2)}) copy-start(bf16[192,256]{1,0:T(8,128)(2,1)S(1)} %collective-permute-done.5.refs_1_) | copy-start | bytes 294916
  48.4 2.4 %copy-start.1 = (bf16[192,256]{1,0:T(8,128)(2,1)}, bf16[192,256]{1,0:T(8,128)(2,1)S(1)}, u32[]{:S(2)}) copy-start(bf16[192,256]{1,0:T(8,128)(2,1)S(1)} %collective-permute-done.6.refs_2_) | copy-start | bytes 294916
  50.8 0.6 %copy-start.2 = (bf16[192,256]{1,0:T(8,128)(2,1)}, bf16[192,256]{1,0:T(8,128)(2,1)S(1)}, u32[]{:S(2)}) copy-start(bf16[192,256]{1,0:T(8,128)(2,1)S(1)} %collective-permute-done.7.refs_3_) | copy-start | bytes 294916

commit v2 on v1

--- a/solution.py
+++ b/solution.py
@@ -15,8 +15,9 @@
 SLOT = 64
 
 BF16, F32 = jnp.bfloat16, jnp.float32
+MIB = 1024 * 1024
 VMEM = pl.BlockSpec(memory_space=pltpu.VMEM)
-ANY = pl.BlockSpec(memory_space=pl.ANY)
+HBM = pl.BlockSpec(memory_space=pltpu.HBM)
 
 
 def place():
@@ -24,13 +25,25 @@
     return lax.rem(position, QUAD), lax.div(position, QUAD)
 
 
-def project_kernel(tap, coarse, weight, bias, *rest):
-    segments, (grid, sparse) = rest[:QUAD], rest[QUAD:]
+def project_kernel(tap_hbm, coarse_hbm, weight_hbm, bias_hbm, *rest):
+    segments, (grid, sparse, tap, coarse, weight, bias, sems) = rest[:QUAD], rest[QUAD:]
     own, _ = place()
+    copies = [
+        pltpu.make_async_copy(source, target, sems.at[i])
+        for i, (source, target) in enumerate(
+            ((weight_hbm, weight), (tap_hbm, tap), (coarse_hbm, coarse), (bias_hbm, bias))
+        )
+    ]
+    for copy in copies:
+        copy.start()
     edge = grid.shape[0] - GW
     grid[0:8] = jnp.zeros((8, grid.shape[1]), F32)
     grid[GW:] = jnp.zeros((edge, grid.shape[1]), F32)
+    copies[0].wait()
+    copies[1].wait()
+    copies[3].wait()
     grid[HALO : HALO + GW] = jnp.dot(tap[...], weight[...], preferred_element_type=F32) + bias[...]
+    copies[2].wait()
     wide = coarse[...].astype(F32)
     sparse[0:8] = jnp.zeros((8, sparse.shape[1]), F32)
     sparse[GW:] = jnp.zeros((edge, sparse.shape[1]), F32)
@@ -308,6 +321,7 @@
     split = proj_weight.shape[1]
     width = out_weight.shape[1]
     shape = jax.ShapeDtypeStruct
+    hbm = functools.partial(pltpu.with_memory_space_constraint, memory_space=pltpu.HBM)
 
     def swap(value, k):
         return lax.ppermute(value, "rows", [(i, i ^ k) for i in range(count)])
@@ -323,10 +337,19 @@
     segments = pl.pallas_call(
         project_kernel,
         out_shape=[shape((SENT, split + width), BF16)] * QUAD,
-        in_specs=[VMEM] * 4,
+        in_specs=[HBM] * 4,
         out_specs=[VMEM] * QUAD,
-        scratch_shapes=[pltpu.VMEM((GW + 16, split), F32), pltpu.VMEM((GW + 16, width), F32)],
-    )(tap_two, coarse_path, proj_weight, proj_bias[None])
+        scratch_shapes=[
+            pltpu.VMEM((GW + 16, split), F32),
+            pltpu.VMEM((GW + 16, width), F32),
+            pltpu.VMEM(tap_two.shape, BF16),
+            pltpu.VMEM(coarse_path.shape, BF16),
+            pltpu.VMEM(proj_weight.shape, BF16),
+            pltpu.VMEM((1, split), F32),
+            pltpu.SemaphoreType.DMA((4,)),
+        ],
+        compiler_params=pltpu.CompilerParams(vmem_limit_bytes=8 * MIB),
+    )(hbm(tap_two), hbm(coarse_path), hbm(proj_weight), hbm(proj_bias[None]))
     segments = [segments[0]] + [swap(segments[k], k) for k in range(1, QUAD)]
     block, first, second = pl.pallas_call(
         functools.partial(pack_kernel, split),
@@ -334,6 +357,7 @@
         + [shape(((HALO + 1) * SENT, split), BF16)] * 2,
         in_specs=[VMEM] * QUAD,
         out_specs=[VMEM] * 3,
+        compiler_params=pltpu.CompilerParams(vmem_limit_bytes=4 * MIB),
     )(*segments)
     first, second = between(first, 0), between(second, 1)
 
@@ -352,7 +376,7 @@
         functools.partial(unite_kernel, blocks),
         out_shape=[shape((4 * SEG, width), BF16)] * QUAD,
         in_specs=[VMEM] * 3
-        + [ANY, VMEM, ANY, ANY, VMEM, ANY, VMEM, ANY, VMEM, ANY, VMEM, ANY, VMEM],
+        + [HBM, VMEM, HBM, HBM, VMEM, HBM, VMEM, HBM, VMEM, HBM, VMEM, HBM, VMEM],
         out_specs=[VMEM] * QUAD,
         scratch_shapes=[pltpu.VMEM(w.shape, BF16) for w in weights]
         + [
@@ -368,24 +392,24 @@
             pltpu.VMEM((width // 128, 4 * QUAD * SEG, 128), F32),
             pltpu.SemaphoreType.DMA((7,)),
         ],
-        compiler_params=pltpu.CompilerParams(vmem_limit_bytes=60 * 1024 * 1024),
+        compiler_params=pltpu.CompilerParams(vmem_limit_bytes=32 * MIB),
         cost_estimate=pl.CostEstimate(flops=flops, bytes_accessed=10_000_000, transcendentals=0),
     )(
         block,
         first,
         second,
-        lift_weight,
+        hbm(lift_weight),
         lift_bias[None],
-        merge_weight,
-        out_weight,
+        hbm(merge_weight),
+        hbm(out_weight),
         out_bias[None],
-        first_inner_w,
+        hbm(first_inner_w),
         first_inner_b[None],
-        first_outer_w,
+        hbm(first_outer_w),
         first_outer_b[None],
-        second_inner_w,
+        hbm(second_inner_w),
         second_inner_b[None],
-        second_outer_w,
+        hbm(second_outer_w),
         second_outer_b[None],
     )
     pieces = [outs[0]] + [swap(outs[k], k) for k in range(1, QUAD)]
@@ -394,6 +418,7 @@
         out_shape=shape((2, 2 * GW, width), BF16),
         in_specs=[VMEM] * QUAD,
         out_specs=VMEM,
+        compiler_params=pltpu.CompilerParams(vmem_limit_bytes=4 * MIB),
     )(*pieces)
 
 

time: 53.7 us -> 45.6 us (0.85)
  Pallas kernels: 26.1 us -> 20.5 us
  local copies, waits for them, and re-layouts: 1.98 us -> 0.02 us
  waiting for transfers between devices: 15.4 us -> 14.7 us
    pallas_call x1, Pallas kernels: 19.8 us -> 17.8 us  [body(): pl.pallas_call(functools.partial(unite_kernel, blocks), out_shape=[shape(...]
    unnamed x16 -> x12, local copies, waits for them, and re-layouts: 1.98 us -> 0.02 us
    pallas_call x1, Pallas kernels: 1.98 us -> 0.09 us  [body(): pl.pallas_call(functools.partial(pack_kernel, split), out_shape=[shape((Q...]
    pallas_call x1, Pallas kernels: 1.82 us -> 0.78 us  [body(): pl.pallas_call(assemble_kernel, out_shape=shape((2, 2 * GW, width), BF16)...]
    pallas_call x1, Pallas kernels: 2.54 us -> 1.85 us  [body(): pl.pallas_call(project_kernel, out_shape=[shape((SENT, split + width), BF...]
where the time goes in v2:
time: 45.6 us; the launch traced here: 45.3 us
  Pallas kernels  20.5 us (45%)
  waiting for transfers between devices  14.7 us (32%)
  starting transfers between devices  9.95 us (22%)
    pallas_call x1, Pallas kernels, body(): pl.pallas_call(functools.partial(unite_kernel, blocks), out_shape=[shape(...  17.8 us
    ppermute x6, waiting for transfers between devices, swap(): return lax.ppermute(value, 'rows', [(i, i ^ k) for i in range(count)])  9.3 us
    ppermute x6, starting transfers between devices, swap(): return lax.ppermute(value, 'rows', [(i, i ^ k) for i in range(count)])  5.4 us
    ppermute x2, waiting for transfers between devices, between(): return lax.ppermute(value, 'rows', pairs)  5.36 us
    ppermute x2, starting transfers between devices, between(): return lax.ppermute(value, 'rows', pairs)  4.55 us
    pallas_call x1, Pallas kernels, body(): pl.pallas_call(project_kernel, out_shape=[shape((SENT, split + width), BF...  1.85 us
  transfers between devices with their start and end apart: 8, of which 6 were waited for; matrix products, arithmetic and copies ran while one was open for 0% of the time, Pallas kernels for 0%

profile of v2, /device:TPU:9, one launch (start us, length us, event | category | flops | bytes accessed | tf_op | source)
XLA Modules:
  0.0 45.3 jit_solution(15771718551726043146)
XLA Ops:
  0.0 0.0 copy-start.2
  0.0 0.0 copy-start.1
  0.0 1.8 %shard_map.163 = (bf16[56,768]{1,0:T(8,128)(2,1)S(1)}, bf16[56,768]{1,0:T(8,128)(2,1)S(1)}, bf16[56,768]{1,0:T(8,128)(2,1)S(1)}, bf16[56,768]{1,0:T(8,128)(2,1)S(1)}) custom-call(bf16[192,1024]{1,0:T(8,128)(2,1)} %tap_hbm.1, bf16[192,256]{1,0:T(8,128)(2,1)} %coarse_hbm.1, bf16[1024,512]{1,0:T(8,128)(2,1)} %weight_hbm.1, f32[1,512]{1,0:T(1,128)} %bitcast.13), custom_call_target="tpu_custom_call" | custom-call | tf_op jit(solution)/shard_map/pallas_call | solution.py:337
  1.9 0.7 %collective-permute-start = (bf16[56,768]{1,0:T(8,128)(2,1)S(1)}, bf16[56,768]{1,0:T(8,128)(2,1)S(1)}, u32[]{:S(2)}, u32[]{:S(2)}) collective-permute-start(bf16[56,768]{1,0:T(8,128)(2,1)S(1)} %get-tuple-element.17), channel_id=1, source_target_pairs={{0,1},{1,0},{2,3},{3,2},{4,5},{5,4},{6,7},{7,6},{8,9},{9,8},{10,11... | collective-permute-start | bytes 258056 | tf_op jit(solution)/shard_map/ppermute | solution.py:327
  2.6 1.2 %collective-permute-start.1 = (bf16[56,768]{1,0:T(8,128)(2,1)S(1)}, bf16[56,768]{1,0:T(8,128)(2,1)S(1)}, u32[]{:S(2)}, u32[]{:S(2)}) collective-permute-start(bf16[56,768]{1,0:T(8,128)(2,1)S(1)} %get-tuple-element.18), channel_id=1, source_target_pairs={{0,2},{1,3},{2,0},{3,1},{4,6},{5,7},{6,4},{7,5},{8,10},{9,11},{10,... | collective-permute-start | bytes 258056 | tf_op jit(solution)/shard_map/ppermute | solution.py:327
  3.9 0.5 %collective-permute-start.2 = (bf16[56,768]{1,0:T(8,128)(2,1)S(1)}, bf16[56,768]{1,0:T(8,128)(2,1)S(1)}, u32[]{:S(2)}, u32[]{:S(2)}) collective-permute-start(bf16[56,768]{1,0:T(8,128)(2,1)S(1)} %get-tuple-element.19), channel_id=1, source_target_pairs={{0,3},{1,2},{2,1},{3,0},{4,7},{5,6},{6,5},{7,4},{8,11},{9,10},{10,... | collective-permute-start | bytes 258056 | tf_op jit(solution)/shard_map/ppermute | solution.py:327
  4.3 0.0 collective-permute-done.refs_1_
  4.3 2.3 %collective-permute-done.1.refs_2_ = bf16[56,768]{1,0:T(8,128)(2,1)S(1)} collective-permute-done((bf16[56,768]{1,0:T(8,128)(2,1)S(1)}, bf16[56,768]{1,0:T(8,128)(2,1)S(1)}, u32[]{:S(2)}, u32[]{:S(2)}) %collective-permute-start.1) | collective-permute-done | bytes 86048 | tf_op jit(solution)/shard_map/ppermute | solution.py:327
  6.6 2.1 %collective-permute-done.2.refs_3_ = bf16[56,768]{1,0:T(8,128)(2,1)S(1)} collective-permute-done((bf16[56,768]{1,0:T(8,128)(2,1)S(1)}, bf16[56,768]{1,0:T(8,128)(2,1)S(1)}, u32[]{:S(2)}, u32[]{:S(2)}) %collective-permute-start.2) | collective-permute-done | bytes 86048 | tf_op jit(solution)/shard_map/ppermute | solution.py:327
  8.7 0.1 shard_map.164
  8.8 0.1 collective-permute-start.3
  8.9 4.4 %collective-permute-start.4 = (bf16[224,512]{1,0:T(8,128)(2,1)S(1)}, bf16[224,512]{1,0:T(8,128)(2,1)S(1)}, u32[]{:S(2)}, u32[]{:S(2)}) collective-permute-start(bf16[224,512]{1,0:T(8,128)(2,1)S(1)} %get-tuple-element.22), channel_id=1, source_target_pairs={{4,8},{8,4},{5,9},{9,5},{6,10},{10,6},{7,11},{11,7},{20,24},{24,20... | collective-permute-start | bytes 688136 | tf_op jit(solution)/shard_map/ppermute | solution.py:335
  13.4 2.4 %collective-permute-done.3.refs_1_ = bf16[224,512]{1,0:T(8,128)(2,1)S(1)} collective-permute-done((bf16[224,512]{1,0:T(8,128)(2,1)S(1)}, bf16[224,512]{1,0:T(8,128)(2,1)S(1)}, u32[]{:S(2)}, u32[]{:S(2)}) %collective-permute-start.3) | collective-permute-done | bytes 229408 | tf_op jit(solution)/shard_map/ppermute | solution.py:335
  15.7 3.0 %collective-permute-done.4.refs_2_ = bf16[224,512]{1,0:T(8,128)(2,1)S(1)} collective-permute-done((bf16[224,512]{1,0:T(8,128)(2,1)S(1)}, bf16[224,512]{1,0:T(8,128)(2,1)S(1)}, u32[]{:S(2)}, u32[]{:S(2)}) %collective-permute-start.4) | collective-permute-done | bytes 229408 | tf_op jit(solution)/shard_map/ppermute | solution.py:335
  18.7 0.0 copy-done.5
  18.8 0.0 copy-done.3
  18.8 17.8 %shard_map.165 = (bf16[192,256]{1,0:T(8,128)(2,1)S(1)}, bf16[192,256]{1,0:T(8,128)(2,1)S(1)}, bf16[192,256]{1,0:T(8,128)(2,1)S(1)}, bf16[192,256]{1,0:T(8,128)(2,1)S(1)}) custom-call(bf16[224,768]{1,0:T(8,128)(2,1)S(1)} %get-tuple-element.20.refs_0_, bf16[224,512]{1,0:T(8,128)(2,1)S(1)} %collective-permute-done.3.refs_1_, ...), custom_call_target="tpu_custom_call" | custom-call | flops 12079595520 | bytes 10000000 | tf_op jit(solution)/shard_map/pallas_call | solution.py:375
  36.6 1.2 %collective-permute-start.5 = (bf16[192,256]{1,0:T(8,128)(2,1)S(1)}, bf16[192,256]{1,0:T(8,128)(2,1)S(1)}, u32[]{:S(2)}, u32[]{:S(2)}) collective-permute-start(bf16[192,256]{1,0:T(8,128)(2,1)S(1)} %get-tuple-element.24), channel_id=1, source_target_pairs={{0,1},{1,0},{2,3},{3,2},{4,5},{5,4},{6,7},{7,6},{8,9},{9,8},{10,11... | collective-permute-start | bytes 294920 | tf_op jit(solution)/shard_map/ppermute | solution.py:327
  37.8 1.3 %collective-permute-start.6 = (bf16[192,256]{1,0:T(8,128)(2,1)S(1)}, bf16[192,256]{1,0:T(8,128)(2,1)S(1)}, u32[]{:S(2)}, u32[]{:S(2)}) collective-permute-start(bf16[192,256]{1,0:T(8,128)(2,1)S(1)} %get-tuple-element.25), channel_id=1, source_target_pairs={{0,2},{1,3},{2,0},{3,1},{4,6},{5,7},{6,4},{7,5},{8,10},{9,11},{10,... | collective-permute-start | bytes 294920 | tf_op jit(solution)/shard_map/ppermute | solution.py:327
  39.1 0.4 collective-permute-start.7
  39.6 0.0 collective-permute-done.5.refs_1_
  39.6 2.6 %collective-permute-done.6.refs_2_ = bf16[192,256]{1,0:T(8,128)(2,1)S(1)} collective-permute-done((bf16[192,256]{1,0:T(8,128)(2,1)S(1)}, bf16[192,256]{1,0:T(8,128)(2,1)S(1)}, u32[]{:S(2)}, u32[]{:S(2)}) %collective-permute-start.6) | collective-permute-done | bytes 98336 | tf_op jit(solution)/shard_map/ppermute | solution.py:327
  42.1 2.4 %collective-permute-done.7.refs_3_ = bf16[192,256]{1,0:T(8,128)(2,1)S(1)} collective-permute-done((bf16[192,256]{1,0:T(8,128)(2,1)S(1)}, bf16[192,256]{1,0:T(8,128)(2,1)S(1)}, u32[]{:S(2)}, u32[]{:S(2)}) %collective-permute-start.7) | collective-permute-done | bytes 98336 | tf_op jit(solution)/shard_map/ppermute | solution.py:327
  44.5 0.8 %shard_map.166 = bf16[2,384,256]{2,1,0:T(8,128)(2,1)} custom-call(bf16[192,256]{1,0:T(8,128)(2,1)S(1)} %get-tuple-element.23.refs_0_, bf16[192,256]{1,0:T(8,128)(2,1)S(1)} %collective-permute-done.5.refs_1_, bf16[192,256]{1,0:T(8,128)(2,1)S(1)} %collective-permute-done.6.refs_2_, bf16[192,256]{1,0:T(8,128)(2,1)S(1)} %collective-permute-done.7.refs_3_), custom_call_target="tpu_custom_call" | custom-call | tf_op jit(solution)/shard_map/pallas_call | solution.py:416
  (8 shorter events, 0.0 us)
Async XLA Ops:
  0.0 18.7 %copy-start.5 = (f32[256]{0:T(256)S(1)}, f32[256]{0:T(256)}, u32[]{:S(2)}) copy-start(f32[256]{0:T(256)} %param.33) | copy-start | bytes 3076
  0.0 18.7 %copy-start.4 = (f32[256]{0:T(256)S(1)}, f32[256]{0:T(256)}, u32[]{:S(2)}) copy-start(f32[256]{0:T(256)} %param.31) | copy-start | bytes 3076
  0.0 18.7 %copy-start.3 = (f32[256]{0:T(256)S(1)}, f32[256]{0:T(256)}, u32[]{:S(2)}) copy-start(f32[256]{0:T(256)} %param.29) | copy-start | bytes 3076
  0.0 18.7 %copy-start.2 = (f32[256]{0:T(256)S(1)}, f32[256]{0:T(256)}, u32[]{:S(2)}) copy-start(f32[256]{0:T(256)} %param.27) | copy-start | bytes 3076
  0.0 18.7 %copy-start.1 = (f32[256]{0:T(256)S(1)}, f32[256]{0:T(256)}, u32[]{:S(2)}) copy-start(f32[256]{0:T(256)} %param.25) | copy-start | bytes 3076
  0.0 18.7 %copy-start = (f32[512]{0:T(512)S(1)}, f32[512]{0:T(512)}, u32[]{:S(2)}) copy-start(f32[512]{0:T(512)} %param.22) | copy-start | bytes 6148
  1.9 2.5 %collective-permute-start = (bf16[56,768]{1,0:T(8,128)(2,1)S(1)}, bf16[56,768]{1,0:T(8,128)(2,1)S(1)}, u32[]{:S(2)}, u32[]{:S(2)}) collective-permute-start(bf16[56,768]{1,0:T(8,128)(2,1)S(1)} %get-tuple-element.17), channel_id=1, source_target_pairs={{0,1},{1,0},{2,3},{3,2},{4,5},{5,4},{6,7},{7,6},{8,9},{9,8},{10,11... | collective-permute-start | bytes 258056 | tf_op jit(solution)/shard_map/ppermute | solution.py:327
  2.6 4.0 %collective-permute-start.1 = (bf16[56,768]{1,0:T(8,128)(2,1)S(1)}, bf16[56,768]{1,0:T(8,128)(2,1)S(1)}, u32[]{:S(2)}, u32[]{:S(2)}) collective-permute-start(bf16[56,768]{1,0:T(8,128)(2,1)S(1)} %get-tuple-element.18), channel_id=1, source_target_pairs={{0,2},{1,3},{2,0},{3,1},{4,6},{5,7},{6,4},{7,5},{8,10},{9,11},{10,... | collective-permute-start | bytes 258056 | tf_op jit(solution)/shard_map/ppermute | solution.py:327
  3.9 4.9 %collective-permute-start.2 = (bf16[56,768]{1,0:T(8,128)(2,1)S(1)}, bf16[56,768]{1,0:T(8,128)(2,1)S(1)}, u32[]{:S(2)}, u32[]{:S(2)}) collective-permute-start(bf16[56,768]{1,0:T(8,128)(2,1)S(1)} %get-tuple-element.19), channel_id=1, source_target_pairs={{0,3},{1,2},{2,1},{3,0},{4,7},{5,6},{6,5},{7,4},{8,11},{9,10},{10,... | collective-permute-start | bytes 258056 | tf_op jit(solution)/shard_map/ppermute | solution.py:327
  8.8 6.9 %collective-permute-start.3 = (bf16[224,512]{1,0:T(8,128)(2,1)S(1)}, bf16[224,512]{1,0:T(8,128)(2,1)S(1)}, u32[]{:S(2)}, u32[]{:S(2)}) collective-permute-start(bf16[224,512]{1,0:T(8,128)(2,1)S(1)} %get-tuple-element.21), channel_id=1, source_target_pairs={{0,4},{4,0},{1,5},{5,1},{2,6},{6,2},{3,7},{7,3},{8,12},{12,8},{9,1... | collective-permute-start | bytes 688136 | tf_op jit(solution)/shard_map/ppermute | solution.py:335
  8.9 9.8 %collective-permute-start.4 = (bf16[224,512]{1,0:T(8,128)(2,1)S(1)}, bf16[224,512]{1,0:T(8,128)(2,1)S(1)}, u32[]{:S(2)}, u32[]{:S(2)}) collective-permute-start(bf16[224,512]{1,0:T(8,128)(2,1)S(1)} %get-tuple-element.22), channel_id=1, source_target_pairs={{4,8},{8,4},{5,9},{9,5},{6,10},{10,6},{7,11},{11,7},{20,24},{24,20... | collective-permute-start | bytes 688136 | tf_op jit(solution)/shard_map/ppermute | solution.py:335
  36.6 3.0 %collective-permute-start.5 = (bf16[192,256]{1,0:T(8,128)(2,1)S(1)}, bf16[192,256]{1,0:T(8,128)(2,1)S(1)}, u32[]{:S(2)}, u32[]{:S(2)}) collective-permute-start(bf16[192,256]{1,0:T(8,128)(2,1)S(1)} %get-tuple-element.24), channel_id=1, source_target_pairs={{0,1},{1,0},{2,3},{3,2},{4,5},{5,4},{6,7},{7,6},{8,9},{9,8},{10,11... | collective-permute-start | bytes 294920 | tf_op jit(solution)/shard_map/ppermute | solution.py:327
  37.8 4.3 %collective-permute-start.6 = (bf16[192,256]{1,0:T(8,128)(2,1)S(1)}, bf16[192,256]{1,0:T(8,128)(2,1)S(1)}, u32[]{:S(2)}, u32[]{:S(2)}) collective-permute-start(bf16[192,256]{1,0:T(8,128)(2,1)S(1)} %get-tuple-element.25), channel_id=1, source_target_pairs={{0,2},{1,3},{2,0},{3,1},{4,6},{5,7},{6,4},{7,5},{8,10},{9,11},{10,... | collective-permute-start | bytes 294920 | tf_op jit(solution)/shard_map/ppermute | solution.py:327
  39.1 5.4 %collective-permute-start.7 = (bf16[192,256]{1,0:T(8,128)(2,1)S(1)}, bf16[192,256]{1,0:T(8,128)(2,1)S(1)}, u32[]{:S(2)}, u32[]{:S(2)}) collective-permute-start(bf16[192,256]{1,0:T(8,128)(2,1)S(1)} %get-tuple-element.26), channel_id=1, source_target_pairs={{0,3},{1,2},{2,1},{3,0},{4,7},{5,6},{6,5},{7,4},{8,11},{9,10},{10,... | collective-permute-start | bytes 294920 | tf_op jit(solution)/shard_map/ppermute | solution.py:327

commit v3 on v2

v3 whole, which is shorter than its diff:
```python
import functools

import jax
import jax.numpy as jnp
from jax import lax
from jax.experimental import pallas as pl
from jax.experimental.pallas import tpu as pltpu
from jax.sharding import PartitionSpec as P

GW = 192
QUAD = 4
SEG = GW // QUAD
HALO = 3
SENT = 56
SLOT = 64

BF16, F32 = jnp.bfloat16, jnp.float32
MIB = 1024 * 1024
VMEM = pl.BlockSpec(memory_space=pltpu.VMEM)
HBM = pl.BlockSpec(memory_space=pltpu.HBM)


def place():
    position = lax.axis_index("rows")
    return lax.rem(position, QUAD), lax.div(position, QUAD)


def project_kernel(tap_hbm, coarse_hbm, weight_hbm, bias_hbm, *rest):
    segments, (grid, sparse, tap, coarse, weight, bias, sems) = rest[:QUAD], rest[QUAD:]
    own, _ = place()
    copies = [
        pltpu.make_async_copy(source, target, sems.at[i])
        for i, (source, target) in enumerate(
            ((weight_hbm, weight), (tap_hbm, tap), (coarse_hbm, coarse), (bias_hbm, bias))
        )
    ]
    for copy in copies:
        copy.start()
    edge = grid.shape[0] - GW
    grid[0:8] = jnp.zeros((8, grid.shape[1]), F32)
    grid[GW:] = jnp.zeros((edge, grid.shape[1]), F32)
    copies[0].wait()
    copies[1].wait()
    copies[3].wait()
    grid[HALO : HALO + GW] = jnp.dot(tap[...], weight[...], preferred_element_type=F32) + bias[...]
    copies[2].wait()
    wide = coarse[...].astype(F32)
    sparse[0:8] = jnp.zeros((8, sparse.shape[1]), F32)
    sparse[GW:] = jnp.zeros((edge, sparse.shape[1]), F32)
    sparse[HALO : HALO + GW] = wide
    sparse[HALO - 1 : HALO] = wide[:1]
    sparse[HALO + GW : HALO + GW + 1] = wide[GW - 1 :]
    split = grid.shape[1]
    for k in range(QUAD):
        start = pl.multiple_of(lax.bitwise_xor(own, k) * SEG, 16)
        segments[k][:, :split] = grid[pl.ds(start, SENT), :].astype(BF16)
        segments[k][:, split:] = sparse[pl.ds(start, SENT), :].astype(BF16)


def pack_kernel(split, *refs):
    segments, (block, first, second) = refs[:QUAD], refs[QUAD:]
    own, number = place()
    for row in range(QUAD):
        for k in range(QUAD):

            @pl.when(own == row ^ k)
            def _():
                block[row * SENT : (row + 1) * SENT] = segments[k][...]

    coarse = block.shape[1] - split
    even = lax.rem(number, 2) == 0

    def fill(payload, row, coarse_row):
        payload[: HALO * SENT] = block[row * SENT : (row + HALO) * SENT, :split]
        for half in range(2):
            payload[HALO * SENT :, half * coarse : (half + 1) * coarse] = block[
                (coarse_row + half) * SENT : (coarse_row + half + 1) * SENT, split:
            ]

    @pl.when(even)
    def _():
        fill(first, 1, 2)
        fill(second, 0, 0)

    @pl.when(jnp.logical_not(even))
    def _():
        fill(first, 0, 0)
        fill(second, 1, 2)


def rows_at(row, rows):
    if isinstance(row, int):
        return pl.ds(row * SLOT, rows * SLOT)
    return pl.ds(pl.multiple_of(row * SLOT, SLOT), rows * SLOT)


def masked(mask, value, row, rows):
    keep = mask[rows_at(row, rows)]
    keep = jnp.concatenate([keep] * (value.shape[1] // 128), axis=1)
    return jnp.where(keep > 0.5, value, 0.0)


def spread_out(target, row, rows, even, odd):
    here, count, width = rows_at(row, rows), rows * SLOT, even.shape[1]
    target[here, :width] = pltpu.roll(odd, 1, 0).astype(BF16)
    target[here, width : 2 * width] = even.astype(BF16)
    target[here, 2 * width : 3 * width] = odd.astype(BF16)
    target[here, 3 * width :] = pltpu.roll(even, count - 1, 0).astype(BF16)


def conv(source, weight, pieces):
    channels = source.shape[1] // 4
    total = None
    for dy in range(3):
        parts = []
        for row, rows in pieces:
            piece = source[rows_at(row + dy, rows)]
            parts += [piece[:, : 3 * channels], piece[:, channels:]]
        part = jnp.dot(
            jnp.concatenate(parts, axis=0),
            weight[3 * dy * channels : 3 * (dy + 1) * channels],
            preferred_element_type=F32,
        )
        total = part if total is None else total + part
    results, at = [], 0
    for _, rows in pieces:
        count = rows * SLOT
        results.append((total[at : at + count], total[at + count : at + 2 * count]))
        at += 2 * count
    return results


def lift(window, weight, bias, mask, target, tokens):
    split = window.shape[1]
    for a in range(2):
        first, lines = tokens[a]
        lhs = window[first * SLOT : (first + len(lines)) * SLOT]
        for b in range(2):
            lifted = jnp.dot(
                lhs,
                weight[:, (2 * a + b) * split : (2 * a + b + 1) * split],
                preferred_element_type=F32,
            )
            plain, moved, shift = (1, 3, SLOT - 1) if b == 0 else (2, 0, 1)
            for i, row in enumerate(lines):
                value = masked(mask, lifted[i * SLOT : (i + 1) * SLOT] + bias[...], row, 1)
                here = rows_at(row, 1)
                target[here, plain * split : (plain + 1) * split] = value.astype(BF16)
                value = pltpu.roll(value, shift, 0).astype(BF16)
                target[here, moved * split : (moved + 1) * split] = value


def enlarged(thin, first, row):
    i, a = divmod(row, 2)
    far = i - 1 if a == 0 else i + 1
    i, far = i - first, far - first
    band = 0.75 * thin[i * SLOT : (i + 1) * SLOT] + 0.25 * thin[far * SLOT : (far + 1) * SLOT]
    left = 0.25 * pltpu.roll(band, 1, 0) + 0.75 * band
    right = 0.75 * band + 0.25 * pltpu.roll(band, SLOT - 1, 0)
    return left, right


def make_reassembled(state, pieces):
    for (row, rows), pair in zip(pieces, conv(state.wide, state.merge_w, pieces), strict=True):
        for parity in range(2):
            state.kept_r[parity, rows_at(row, rows)] = pair[parity].astype(BF16)
        pair = [masked(state.mask, jnp.maximum(v, 0.0), row + 1, rows) for v in pair]
        spread_out(state.x_r, row, rows, *pair)


def make_inner(source, weight, bias, mask, target, offset, pieces):
    for (row, rows), pair in zip(pieces, conv(source, weight, pieces), strict=True):
        pair = [masked(mask, jnp.maximum(v + bias[...], 0.0), row + offset, rows) for v in pair]
        spread_out(target, row, rows, *pair)


def make_merged(state, carried, pieces):
    bias = state.outer1_b[...] + state.out_b[...]
    for (row, rows), pair in zip(pieces, conv(state.x_i, state.outer1_w, pieces), strict=True):
        done = []
        for parity in range(2):
            old = state.kept_r[parity, rows_at(row + 2, rows)].astype(F32)
            value = pair[parity] + bias + old + carried(parity, row, rows)
            state.kept_m[parity, rows_at(row, rows)] = value.astype(BF16)
            done.append(masked(state.mask, jnp.maximum(value, 0.0), row + 3, rows))
        spread_out(state.x_m, row, rows, *done)


def make_united(state, fine, row, outs):
    own, _ = place()
    pair = conv(state.x_n, state.outer2_w, [(row, 4)])[0]
    for parity in range(2):
        old = state.kept_m[parity, rows_at(row + 2, 4)].astype(F32)
        value = pair[parity] + state.outer2_b[...] + old
        for r in range(4):
            cells = value[r * SLOT + HALO : r * SLOT + HALO + SEG]
            for half in range(fine.shape[0]):
                fine[half, pl.ds(r * 2 * SEG + parity, SEG, 2), :] = cells[
                    :, half * 128 : (half + 1) * 128
                ]
    core = lax.rem(own, 2)
    for j in range(2):
        start = pl.multiple_of(lax.bitwise_xor(core, j) * (4 * SEG), 16)
        for half in range(fine.shape[0]):
            value = fine[half, pl.ds(start, 4 * SEG), :].astype(BF16)
            outs[j][:, half * 128 : (half + 1) * 128] = value


class Named:
    def __init__(self, names, refs):
        for name, ref in zip(names, refs, strict=True):
            setattr(self, name, ref)


WEIGHTS = ("lift_w", "merge_w", "inner1_w", "out_w", "outer1_w", "inner2_w", "outer2_w")
BIASES = ("lift_b", "out_b", "inner1_b", "outer1_b", "inner2_b", "outer2_b")
ARRAYS = ("mask", "wide", "x_r", "x_i", "x_m", "kept_r", "kept_m")
LATER = ("x_n", "even_c", "odd_c")


def inner_kernel(blocks, *refs):
    n = len(WEIGHTS)
    block, sources, biases = refs[0], refs[1 : 1 + n], refs[1 + n : 7 + n]
    outs = refs[7 + n : 7 + n + len(ARRAYS) + n]
    window, coarse, thin, sems = refs[-4:]
    state = Named(BIASES + ARRAYS + WEIGHTS, biases + outs)
    own, number = place()
    split = window.shape[1]
    copies = {}
    for i, (name, source) in enumerate(zip(WEIGHTS, sources, strict=True)):
        copies[name] = pltpu.make_async_copy(source, getattr(state, name), sems.at[i])
        copies[name].start()

    slot = lax.broadcasted_iota(jnp.int32, (SLOT, 128), 0)
    token = slot + (own * SEG - HALO)
    inside = (token >= 0) & (token < GW) & (slot < SEG + 2 * HALO)
    inside = jnp.where(inside, 1.0, 0.0)
    for r in range(2 * QUAD + 10):
        at = number * (2 * QUAD) + (r - 5)
        good = jnp.where((at >= 0) & (at < blocks * 2 * QUAD), 1.0, 0.0)
        state.mask[r * SLOT : (r + 1) * SLOT] = inside * good

    for i in range(QUAD):
        there = slice(i * SENT, (i + 1) * SENT)
        for target, cols in ((window, slice(0, split)), (coarse, slice(split, None))):
            target[i * SLOT : i * SLOT + SENT] = block[there, cols]
            blank = jnp.zeros((SLOT - SENT, target.shape[1]), BF16)
            target[i * SLOT + SENT : (i + 1) * SLOT] = blank

    copies["lift_w"].wait()
    tokens = [(0, [5 + 2 * i + a for i in range(QUAD)]) for a in range(2)]
    lift(window, state.lift_w, state.lift_b, state.mask, state.wide, tokens)
    copies["merge_w"].wait()
    make_reassembled(state, [(5, 6)])
    copies["inner1_w"].wait()
    make_inner(state.x_r, state.inner1_w, state.inner1_b, state.mask, state.x_i, 2, [(5, 4)])
    copies["out_w"].wait()
    thin[...] = jnp.dot(coarse[...], state.out_w[...], preferred_element_type=F32)
    copies["outer1_w"].wait()

    def carried(parity, row, rows):
        return jnp.concatenate([enlarged(thin, 0, r - 2)[parity] for r in range(row, row + rows)])

    make_merged(state, carried, [(5, 2)])
    copies["inner2_w"].wait()
    copies["outer2_w"].wait()


def near_kernel(blocks, *refs):
    names = BIASES + WEIGHTS + tuple("old_" + name for name in ARRAYS)
    block, first, second = refs[:3]
    inputs = refs[3 : 3 + len(names)]
    outs = refs[3 + len(names) : -4]
    window, coarse, thin, fine = refs[-4:]
    state = Named(names + ARRAYS + LATER, inputs + outs[: len(ARRAYS) + len(LATER)])
    results = outs[len(ARRAYS) + len(LATER) :]
    own, number = place()
    split, width = window.shape[1], thin.shape[1]

    for target in (window, coarse):
        blank = jnp.zeros((SLOT - SENT, target.shape[1]), BF16)
        for i in range(target.shape[0] // SLOT):
            target[i * SLOT + SENT : (i + 1) * SLOT] = blank
    for i in range(QUAD):
        at = (i + 2) * SLOT
        coarse[at : at + SENT] = block[i * SENT : (i + 1) * SENT, split:]

    def land(payload, row, coarse_row):
        for i in range(HALO):
            at = (row + i) * SLOT
            window[at : at + SENT] = payload[i * SENT : (i + 1) * SENT]
        for half in range(2):
            at = (coarse_row + half) * SLOT
            coarse[at : at + SENT] = payload[HALO * SENT :, half * width : (half + 1) * width]

    even_block = lax.rem(number, 2) == 0

    @pl.when(even_block)
    def _():
        land(second, 0, 0)
        land(first, HALO, QUAD + 2)

    @pl.when(jnp.logical_not(even_block))
    def _():
        land(first, 0, 0)
        land(second, HALO, QUAD + 2)

    @pl.when(number == 0)
    def _():
        coarse[SLOT : SLOT + SENT] = block[:SENT, split:]

    @pl.when(number == blocks - 1)
    def _():
        at = (QUAD + 2) * SLOT
        coarse[at : at + SENT] = block[(QUAD - 1) * SENT :, split:]

    tokens = [(1, [1, 3, 13, 15, 17]), (0, [0, 2, 4, 14, 16])]
    lift(window, state.lift_w, state.lift_b, state.mask, state.wide, tokens)
    thin[...] = jnp.dot(coarse[...], state.out_w[...], preferred_element_type=F32)
    for row in range(2 * QUAD + 4):
        left, right = enlarged(thin, -2, row - 2)
        state.even_c[row * SLOT : (row + 1) * SLOT] = left
        state.odd_c[row * SLOT : (row + 1) * SLOT] = right

    def carried(parity, row, rows):
        return (state.even_c, state.odd_c)[parity][rows_at(row, rows)]

    other = 1 - lax.div(own, 2)
    single, run = 11 - 7 * other, 11 * other
    pieces = [(single, 1), (run, 5)]
    make_reassembled(state, pieces)
    pieces = [(9 - 5 * other, 1), (9 * other, 5)]
    make_inner(state.x_r, state.inner1_w, state.inner1_b, state.mask, state.x_i, 2, pieces)
    pieces = [(7 - 3 * other, 1), (7 * other, 5)]
    make_merged(state, carried, pieces)
    pieces = [(4 * other, 6)]
    make_inner(state.x_m, state.inner2_w, state.inner2_b, state.mask, state.x_n, 4, pieces)
    make_united(state, fine, 4 * other, results)


def own_kernel(*refs):
    arrays = ARRAYS + LATER
    names = BIASES + WEIGHTS + tuple("old_" + name for name in arrays)
    inputs, outs, fine = refs[: len(names)], refs[len(names) : -1], refs[-1]
    state = Named(names + arrays, inputs + outs[: len(arrays)])
    own, _ = place()

    def carried(parity, row, rows):
        return (state.even_c, state.odd_c)[parity][rows_at(row, rows)]

    mine = lax.div(own, 2)
    make_reassembled(state, [(12 * mine, 4)])
    pieces = [(10 * mine, 4)]
    make_inner(state.x_r, state.inner1_w, state.inner1_b, state.mask, state.x_i, 2, pieces)
    make_merged(state, carried, [(8 * mine, 4)])
    pieces = [(6 * mine, 4)]
    make_inner(state.x_m, state.inner2_w, state.inner2_b, state.mask, state.x_n, 4, pieces)
    make_united(state, fine, 4 * mine, outs[len(arrays) :])


def assemble_kernel(*refs):
    pieces, out = refs[:QUAD], refs[QUAD]
    own, _ = place()
    for k in range(QUAD):
        start = pl.multiple_of(lax.bitwise_xor(own, k) * (2 * SEG), 16)
        for r in range(2):
            out[r, pl.ds(start, 2 * SEG), :] = pieces[k][r * 2 * SEG : (r + 1) * 2 * SEG]


def body(
    tap_two,
    coarse_path,
    proj_weight,
    proj_bias,
    lift_weight,
    lift_bias,
    merge_weight,
    out_weight,
    out_bias,
    first_inner_w,
    first_inner_b,
    first_outer_w,
    first_outer_b,
    second_inner_w,
    second_inner_b,
    second_outer_w,
    second_outer_b,
):
    count = lax.axis_size("rows")
    if tap_two.shape[0] != GW or count % QUAD:
        raise ValueError("unsupported split")
    blocks = count // QUAD
    split = proj_weight.shape[1]
    width = out_weight.shape[1]
    shape = jax.ShapeDtypeStruct
    hbm = functools.partial(pltpu.with_memory_space_constraint, memory_space=pltpu.HBM)

    def swap(value, k):
        return lax.ppermute(value, "rows", [(i, i ^ k) for i in range(count)])

    def between(value, parity):
        pairs = []
        for low in range(parity, blocks - 1, 2):
            for q in range(QUAD):
                a, b = low * QUAD + q, (low + 1) * QUAD + q
                pairs += [(a, b), (b, a)]
        return lax.ppermute(value, "rows", pairs)

    segments = pl.pallas_call(
        project_kernel,
        out_shape=[shape((SENT, split + width), BF16)] * QUAD,
        in_specs=[HBM] * 4,
        out_specs=[VMEM] * QUAD,
        scratch_shapes=[
            pltpu.VMEM((GW + 16, split), F32),
            pltpu.VMEM((GW + 16, width), F32),
            pltpu.VMEM(tap_two.shape, BF16),
            pltpu.VMEM(coarse_path.shape, BF16),
            pltpu.VMEM(proj_weight.shape, BF16),
            pltpu.VMEM((1, split), F32),
            pltpu.SemaphoreType.DMA((4,)),
        ],
        compiler_params=pltpu.CompilerParams(vmem_limit_bytes=8 * MIB),
    )(hbm(tap_two), hbm(coarse_path), hbm(proj_weight), hbm(proj_bias[None]))
    segments = [segments[0]] + [swap(segments[k], k) for k in range(1, QUAD)]
    block, first, second = pl.pallas_call(
        functools.partial(pack_kernel, split),
        out_shape=[shape((QUAD * SENT, split + width), BF16)]
        + [shape(((HALO + 1) * SENT, split), BF16)] * 2,
        in_specs=[VMEM] * QUAD,
        out_specs=[VMEM] * 3,
        compiler_params=pltpu.CompilerParams(vmem_limit_bytes=4 * MIB),
    )(*segments)
    first, second = between(first, 0), between(second, 1)

    weights = (
        lift_weight,
        merge_weight,
        first_inner_w,
        out_weight,
        first_outer_w,
        second_inner_w,
        second_outer_w,
    )
    biases = (lift_bias, out_bias, first_inner_b, first_outer_b, second_inner_b, second_outer_b)
    biases = [bias[None] for bias in biases]
    rows_w = 2 * QUAD + 10
    arrays = [
        pltpu.VMEM((rows_w * SLOT, 128), F32),
        pltpu.VMEM((rows_w * SLOT, 4 * split), BF16),
        pltpu.VMEM(((rows_w - 2) * SLOT, 4 * width), BF16),
        pltpu.VMEM(((rows_w - 4) * SLOT, 4 * width), BF16),
        pltpu.VMEM(((rows_w - 6) * SLOT, 4 * width), BF16),
        pltpu.VMEM((2, (rows_w - 2) * SLOT, width), BF16),
        pltpu.VMEM((2, (rows_w - 6) * SLOT, width), BF16),
    ]
    later = [
        pltpu.VMEM(((rows_w - 8) * SLOT, 4 * width), BF16),
        pltpu.VMEM(((rows_w - 6) * SLOT, width), F32),
        pltpu.VMEM(((rows_w - 6) * SLOT, width), F32),
    ]
    results = [shape((4 * SEG, width), BF16)] * 2

    def cost(lift_rows, merge_rows, rest_rows):
        cells = 2 * SLOT * 2 * split * lift_rows * split
        cells += 2 * 2 * SLOT * 9 * width * (split * merge_rows + width * rest_rows)
        return pl.CostEstimate(flops=cells, bytes_accessed=1_000_000, transcendentals=0)

    def limit(mib):
        return pltpu.CompilerParams(vmem_limit_bytes=mib * MIB)

    made = pl.pallas_call(
        functools.partial(inner_kernel, blocks),
        out_shape=arrays + [pltpu.VMEM(w.shape, BF16) for w in weights],
        in_specs=[VMEM] + [HBM] * len(weights) + [VMEM] * len(biases),
        out_specs=[VMEM] * (len(arrays) + len(weights)),
        scratch_shapes=[
            pltpu.VMEM((QUAD * SLOT, split), BF16),
            pltpu.VMEM((QUAD * SLOT, width), BF16),
            pltpu.VMEM((QUAD * SLOT, width), F32),
            pltpu.SemaphoreType.DMA((len(weights),)),
        ],
        compiler_params=limit(16),
        cost_estimate=cost(8, 6, 6),
    )(block, *[hbm(w) for w in weights], *biases)
    made, weights = made[: len(arrays)], made[len(arrays) :]
    before = 3 + len(biases) + len(weights)
    made = pl.pallas_call(
        functools.partial(near_kernel, blocks),
        out_shape=arrays + later + results,
        in_specs=[VMEM] * (before + len(arrays)),
        out_specs=[VMEM] * (len(arrays) + len(later) + 2),
        scratch_shapes=[
            pltpu.VMEM((2 * HALO * SLOT, split), BF16),
            pltpu.VMEM(((QUAD + 4) * SLOT, width), BF16),
            pltpu.VMEM(((QUAD + 4) * SLOT, width), F32),
            pltpu.VMEM((width // 128, 8 * SEG, 128), F32),
        ],
        input_output_aliases={before + i: i for i in range(len(arrays))},
        compiler_params=limit(16),
        cost_estimate=cost(10, 6, 22),
    )(block, first, second, *biases, *weights, *made)
    arrays += later
    made, far = made[:-2], made[-2:]
    far = [swap(far[j], 2 + j) for j in range(2)]
    before = len(biases) + len(weights)
    made = pl.pallas_call(
        own_kernel,
        out_shape=arrays + results,
        in_specs=[VMEM] * (before + len(arrays)),
        out_specs=[VMEM] * (len(arrays) + 2),
        scratch_shapes=[pltpu.VMEM((width // 128, 8 * SEG, 128), F32)],
        input_output_aliases={before + i: i for i in range(len(arrays))},
        compiler_params=limit(16),
        cost_estimate=cost(0, 4, 16),
    )(*biases, *weights, *made)
    pieces = [made[-2], swap(made[-1], 1), *far]
    return pl.pallas_call(
        assemble_kernel,
        out_shape=shape((2, 2 * GW, width), BF16),
        in_specs=[VMEM] * QUAD,
        out_specs=VMEM,
        compiler_params=pltpu.CompilerParams(vmem_limit_bytes=4 * MIB),
    )(*pieces)


def solution(mesh):
    return jax.shard_map(
        body,
        mesh=mesh,
        in_specs=(P(("groups", "rows"), None), P(("groups", "rows"), None)) + (P(),) * 15,
        out_specs=P(("groups", "rows"), None, None),
        check_vma=False,
    )
```

time: 45.6 us -> 50.6 us (1.11)
  Pallas kernels: 20.5 us -> 31.3 us
  waiting for transfers between devices: 14.7 us -> 9.31 us
    pallas_call x1 -> x3, Pallas kernels: 17.8 us -> 28.6 us  [the longest x1 12.7 us: body(): pl.pallas_call(functools.partial(near_kernel, blocks), out_shape=arrays +...]
    ppermute x2, waiting for transfers between devices: 5.36 us -> 0.01 us  [between(): return lax.ppermute(value, 'rows', pairs)]
  transfers between devices with their start and end apart: 8 -> 8, of which waited for: 6 -> 4; matrix products, arithmetic and copies ran while one was open for 0% -> 0% of each run, Pallas kernels for 0% -> 16%
where the time goes in v3:
time: 50.6 us; the launch traced here: 50.4 us
  Pallas kernels  31.3 us (62%)
  starting transfers between devices  9.64 us (19%)
  waiting for transfers between devices  9.31 us (18%)
    pallas_call x1, Pallas kernels, body(): pl.pallas_call(functools.partial(near_kernel, blocks), out_shape=arrays +...  12.7 us
    ppermute x6, waiting for transfers between devices, swap(): return lax.ppermute(value, 'rows', [(i, i ^ k) for i in range(count)])  9.3 us
    pallas_call x1, Pallas kernels, body(): pl.pallas_call(own_kernel, out_shape=arrays + results, in_specs=[VMEM] *...  8.05 us
    pallas_call x1, Pallas kernels, body(): pl.pallas_call(functools.partial(inner_kernel, blocks), out_shape=arrays...  7.87 us
    ppermute x6, starting transfers between devices, swap(): return lax.ppermute(value, 'rows', [(i, i ^ k) for i in range(count)])  5.08 us
    ppermute x2, starting transfers between devices, between(): return lax.ppermute(value, 'rows', pairs)  4.56 us
    pallas_call x1, Pallas kernels, body(): pl.pallas_call(project_kernel, out_shape=[shape((SENT, split + width), BF...  1.84 us
  transfers between devices with their start and end apart: 8, of which 4 were waited for; matrix products, arithmetic and copies ran while one was open for 0% of the time, Pallas kernels for 16%

profile of v3, /device:TPU:9, one launch (start us, length us, event | category | flops | bytes accessed | tf_op | source)
XLA Modules:
  0.0 50.4 jit_solution(10788344071300011323)
XLA Ops:
  0.0 1.8 %shard_map.163 = (bf16[56,768]{1,0:T(8,128)(2,1)S(1)}, bf16[56,768]{1,0:T(8,128)(2,1)S(1)}, bf16[56,768]{1,0:T(8,128)(2,1)S(1)}, bf16[56,768]{1,0:T(8,128)(2,1)S(1)}) custom-call(bf16[192,1024]{1,0:T(8,128)(2,1)} %tap_hbm.1, bf16[192,256]{1,0:T(8,128)(2,1)} %coarse_hbm.1, bf16[1024,512]{1,0:T(8,128)(2,1)} %weight_hbm.1, f32[1,512]{1,0:T(1,128)} %bitcast.25), custom_call_target="tpu_custom_call" | custom-call | tf_op jit(solution)/shard_map/pallas_call | solution.py:409
  1.9 0.7 %collective-permute-start = (bf16[56,768]{1,0:T(8,128)(2,1)S(1)}, bf16[56,768]{1,0:T(8,128)(2,1)S(1)}, u32[]{:S(2)}, u32[]{:S(2)}) collective-permute-start(bf16[56,768]{1,0:T(8,128)(2,1)S(1)} %get-tuple-element.41), channel_id=1, source_target_pairs={{0,1},{1,0},{2,3},{3,2},{4,5},{5,4},{6,7},{7,6},{8,9},{9,8},{10,11... | collective-permute-start | bytes 258056 | tf_op jit(solution)/shard_map/ppermute | solution.py:399
  2.6 1.2 %collective-permute-start.1 = (bf16[56,768]{1,0:T(8,128)(2,1)S(1)}, bf16[56,768]{1,0:T(8,128)(2,1)S(1)}, u32[]{:S(2)}, u32[]{:S(2)}) collective-permute-start(bf16[56,768]{1,0:T(8,128)(2,1)S(1)} %get-tuple-element.42), channel_id=1, source_target_pairs={{0,2},{1,3},{2,0},{3,1},{4,6},{5,7},{6,4},{7,5},{8,10},{9,11},{10,... | collective-permute-start | bytes 258056 | tf_op jit(solution)/shard_map/ppermute | solution.py:399
  3.9 0.5 collective-permute-start.2
  4.3 0.0 collective-permute-done.refs_1_
  4.3 2.3 %collective-permute-done.1.refs_2_ = bf16[56,768]{1,0:T(8,128)(2,1)S(1)} collective-permute-done((bf16[56,768]{1,0:T(8,128)(2,1)S(1)}, bf16[56,768]{1,0:T(8,128)(2,1)S(1)}, u32[]{:S(2)}, u32[]{:S(2)}) %collective-permute-start.1) | collective-permute-done | bytes 86048 | tf_op jit(solution)/shard_map/ppermute | solution.py:399
  6.6 2.1 %collective-permute-done.2.refs_3_ = bf16[56,768]{1,0:T(8,128)(2,1)S(1)} collective-permute-done((bf16[56,768]{1,0:T(8,128)(2,1)S(1)}, bf16[56,768]{1,0:T(8,128)(2,1)S(1)}, u32[]{:S(2)}, u32[]{:S(2)}) %collective-permute-start.2) | collective-permute-done | bytes 86048 | tf_op jit(solution)/shard_map/ppermute | solution.py:399
  8.7 0.1 shard_map.164
  8.8 0.1 collective-permute-start.3
  8.9 4.4 %collective-permute-start.4 = (bf16[224,512]{1,0:T(8,128)(2,1)S(1)}, bf16[224,512]{1,0:T(8,128)(2,1)S(1)}, u32[]{:S(2)}, u32[]{:S(2)}) collective-permute-start(bf16[224,512]{1,0:T(8,128)(2,1)S(1)} %get-tuple-element.53), channel_id=1, source_target_pairs={{4,8},{8,4},{5,9},{9,5},{6,10},{10,6},{7,11},{11,7},{20,24},{24,20... | collective-permute-start | bytes 688136 | tf_op jit(solution)/shard_map/ppermute | solution.py:407
  13.4 0.0 copy-done.5
  13.4 0.0 copy-done.4
  13.4 7.9 %shard_map.165 = (f32[1152,128]{1,0:T(8,128)S(1)}, bf16[1152,2048]{1,0:T(8,128)(2,1)S(1)}, bf16[1024,1024]{1,0:T(8,128)(2,1)S(1)}, bf16[896,1024]{1,0:T(8,128)(2...) custom-call(bf16[224,768]{1,0:T(8,128)(2,1)S(1)} %get-tuple-element., ...), custom_call_target="tpu_custom_call" | custom-call | flops 3254779904 | bytes 1000000 | tf_op jit(solution)/shard_map/pallas_call | solution.py:472
  21.3 0.0 collective-permute-done.3.refs_1_
  21.3 0.0 collective-permute-done.4.refs_2_
  21.3 12.7 %shard_map.166 = (f32[1152,128]{1,0:T(8,128)S(1)}, bf16[1152,2048]{1,0:T(8,128)(2,1)S(1)}, bf16[1024,1024]{1,0:T(8,128)(2,1)S(1)}, bf16[896,1024]{1,0:T(8,128)(2...) custom-call(bf16[224,768]{1,0:T(8,128)(2,1)S(1)} %get-tuple-element., ...), custom_call_target="tpu_custom_call", output_to_operand_aliasing={{0}: (16, {}), {1}: (17, {}), {2}: (18, {}), {3}: (19, {}),... | custom-call | flops 5804916736 | bytes 1000000 | tf_op jit(solution)/shard_map/pallas_call | solution.py:488
  34.0 8.1 %shard_map.167 = (f32[1152,128]{1,0:T(8,128)S(1)}, bf16[1152,2048]{1,0:T(8,128)(2,1)S(1)}, bf16[1024,1024]{1,0:T(8,128)(2,1)S(1)}, bf16[896,1024]{1,0:T(8,128)(2...) custom-call(f32[1,512]{1,0:T(1,128)S(1)} %bitcast.9, ...), custom_call_target="tpu_custom_call", output_to_operand_aliasing={{0}: (13, {}), {1}: (14, {}), {2}: (15, {}), {3}: (16, {}),... | custom-call | flops 3623878656 | bytes 1000000 | tf_op jit(solution)/shard_map/pallas_call | solution.py:507
  42.1 0.9 %collective-permute-start.5 = (bf16[192,256]{1,0:T(8,128)(2,1)S(1)}, bf16[192,256]{1,0:T(8,128)(2,1)S(1)}, u32[]{:S(2)}, u32[]{:S(2)}) collective-permute-start(bf16[192,256]{1,0:T(8,128)(2,1)S(1)} %get-tuple-element.72), channel_id=1, source_target_pairs={{0,1},{1,0},{2,3},{3,2},{4,5},{5,4},{6,7},{7,6},{8,9},{9,8},{10,11... | collective-permute-start | bytes 294920 | tf_op jit(solution)/shard_map/ppermute | solution.py:399
  43.0 1.1 %collective-permute-start.6 = (bf16[192,256]{1,0:T(8,128)(2,1)S(1)}, bf16[192,256]{1,0:T(8,128)(2,1)S(1)}, u32[]{:S(2)}, u32[]{:S(2)}) collective-permute-start(bf16[192,256]{1,0:T(8,128)(2,1)S(1)} %get-tuple-element.73), channel_id=1, source_target_pairs={{0,2},{1,3},{2,0},{3,1},{4,6},{5,7},{6,4},{7,5},{8,10},{9,11},{10,... | collective-permute-start | bytes 294920 | tf_op jit(solution)/shard_map/ppermute | solution.py:399
  44.0 0.7 %collective-permute-start.7 = (bf16[192,256]{1,0:T(8,128)(2,1)S(1)}, bf16[192,256]{1,0:T(8,128)(2,1)S(1)}, u32[]{:S(2)}, u32[]{:S(2)}) collective-permute-start(bf16[192,256]{1,0:T(8,128)(2,1)S(1)} %get-tuple-element.74), channel_id=1, source_target_pairs={{0,3},{1,2},{2,1},{3,0},{4,7},{5,6},{6,5},{7,4},{8,11},{9,10},{10,... | collective-permute-start | bytes 294920 | tf_op jit(solution)/shard_map/ppermute | solution.py:399
  44.7 0.0 collective-permute-done.5.refs_1_
  44.7 2.6 %collective-permute-done.6.refs_2_ = bf16[192,256]{1,0:T(8,128)(2,1)S(1)} collective-permute-done((bf16[192,256]{1,0:T(8,128)(2,1)S(1)}, bf16[192,256]{1,0:T(8,128)(2,1)S(1)}, u32[]{:S(2)}, u32[]{:S(2)}) %collective-permute-start.6) | collective-permute-done | bytes 98336 | tf_op jit(solution)/shard_map/ppermute | solution.py:399
  47.3 2.4 %collective-permute-done.7.refs_3_ = bf16[192,256]{1,0:T(8,128)(2,1)S(1)} collective-permute-done((bf16[192,256]{1,0:T(8,128)(2,1)S(1)}, bf16[192,256]{1,0:T(8,128)(2,1)S(1)}, u32[]{:S(2)}, u32[]{:S(2)}) %collective-permute-start.7) | collective-permute-done | bytes 98336 | tf_op jit(solution)/shard_map/ppermute | solution.py:399
  49.6 0.8 %shard_map.168 = bf16[2,384,256]{2,1,0:T(8,128)(2,1)} custom-call(bf16[192,256]{1,0:T(8,128)(2,1)S(1)} %get-tuple-element.71.refs_0_, bf16[192,256]{1,0:T(8,128)(2,1)S(1)} %collective-permute-done.5.refs_1_, bf16[192,256]{1,0:T(8,128)(2,1)S(1)} %collective-permute-done.6.refs_2_, bf16[192,256]{1,0:T(8,128)(2,1)S(1)} %collective-permute-done.7.refs_3_), custom_call_target="tpu_custom_call" | custom-call | tf_op jit(solution)/shard_map/pallas_call | solution.py:518
  (10 shorter events, 0.0 us)
Async XLA Ops:
  0.0 13.4 %copy-start.5 = (f32[256]{0:T(256)S(1)}, f32[256]{0:T(256)}, u32[]{:S(2)}) copy-start(f32[256]{0:T(256)} %param.33) | copy-start | bytes 3076
  0.0 13.4 %copy-start.4 = (f32[256]{0:T(256)S(1)}, f32[256]{0:T(256)}, u32[]{:S(2)}) copy-start(f32[256]{0:T(256)} %param.31) | copy-start | bytes 3076
  0.0 13.4 %copy-start.3 = (f32[256]{0:T(256)S(1)}, f32[256]{0:T(256)}, u32[]{:S(2)}) copy-start(f32[256]{0:T(256)} %param.29) | copy-start | bytes 3076
  0.0 13.4 %copy-start.2 = (f32[256]{0:T(256)S(1)}, f32[256]{0:T(256)}, u32[]{:S(2)}) copy-start(f32[256]{0:T(256)} %param.27) | copy-start | bytes 3076
  0.0 13.4 %copy-start.1 = (f32[256]{0:T(256)S(1)}, f32[256]{0:T(256)}, u32[]{:S(2)}) copy-start(f32[256]{0:T(256)} %param.25) | copy-start | bytes 3076
  0.0 13.4 %copy-start = (f32[512]{0:T(512)S(1)}, f32[512]{0:T(512)}, u32[]{:S(2)}) copy-start(f32[512]{0:T(512)} %param.22) | copy-start | bytes 6148
  1.9 2.5 %collective-permute-start = (bf16[56,768]{1,0:T(8,128)(2,1)S(1)}, bf16[56,768]{1,0:T(8,128)(2,1)S(1)}, u32[]{:S(2)}, u32[]{:S(2)}) collective-permute-start(bf16[56,768]{1,0:T(8,128)(2,1)S(1)} %get-tuple-element.41), channel_id=1, source_target_pairs={{0,1},{1,0},{2,3},{3,2},{4,5},{5,4},{6,7},{7,6},{8,9},{9,8},{10,11... | collective-permute-start | bytes 258056 | tf_op jit(solution)/shard_map/ppermute | solution.py:399
  2.6 4.0 %collective-permute-start.1 = (bf16[56,768]{1,0:T(8,128)(2,1)S(1)}, bf16[56,768]{1,0:T(8,128)(2,1)S(1)}, u32[]{:S(2)}, u32[]{:S(2)}) collective-permute-start(bf16[56,768]{1,0:T(8,128)(2,1)S(1)} %get-tuple-element.42), channel_id=1, source_target_pairs={{0,2},{1,3},{2,0},{3,1},{4,6},{5,7},{6,4},{7,5},{8,10},{9,11},{10,... | collective-permute-start | bytes 258056 | tf_op jit(solution)/shard_map/ppermute | solution.py:399
  3.9 4.9 %collective-permute-start.2 = (bf16[56,768]{1,0:T(8,128)(2,1)S(1)}, bf16[56,768]{1,0:T(8,128)(2,1)S(1)}, u32[]{:S(2)}, u32[]{:S(2)}) collective-permute-start(bf16[56,768]{1,0:T(8,128)(2,1)S(1)} %get-tuple-element.43), channel_id=1, source_target_pairs={{0,3},{1,2},{2,1},{3,0},{4,7},{5,6},{6,5},{7,4},{8,11},{9,10},{10,... | collective-permute-start | bytes 258056 | tf_op jit(solution)/shard_map/ppermute | solution.py:399
  8.8 12.5 %collective-permute-start.3 = (bf16[224,512]{1,0:T(8,128)(2,1)S(1)}, bf16[224,512]{1,0:T(8,128)(2,1)S(1)}, u32[]{:S(2)}, u32[]{:S(2)}) collective-permute-start(bf16[224,512]{1,0:T(8,128)(2,1)S(1)} %get-tuple-element.52), channel_id=1, source_target_pairs={{0,4},{4,0},{1,5},{5,1},{2,6},{6,2},{3,7},{7,3},{8,12},{12,8},{9,1... | collective-permute-start | bytes 688136 | tf_op jit(solution)/shard_map/ppermute | solution.py:407
  8.9 12.4 %collective-permute-start.4 = (bf16[224,512]{1,0:T(8,128)(2,1)S(1)}, bf16[224,512]{1,0:T(8,128)(2,1)S(1)}, u32[]{:S(2)}, u32[]{:S(2)}) collective-permute-start(bf16[224,512]{1,0:T(8,128)(2,1)S(1)} %get-tuple-element.53), channel_id=1, source_target_pairs={{4,8},{8,4},{5,9},{9,5},{6,10},{10,6},{7,11},{11,7},{20,24},{24,20... | collective-permute-start | bytes 688136 | tf_op jit(solution)/shard_map/ppermute | solution.py:407
  42.1 2.6 %collective-permute-start.5 = (bf16[192,256]{1,0:T(8,128)(2,1)S(1)}, bf16[192,256]{1,0:T(8,128)(2,1)S(1)}, u32[]{:S(2)}, u32[]{:S(2)}) collective-permute-start(bf16[192,256]{1,0:T(8,128)(2,1)S(1)} %get-tuple-element.72), channel_id=1, source_target_pairs={{0,1},{1,0},{2,3},{3,2},{4,5},{5,4},{6,7},{7,6},{8,9},{9,8},{10,11... | collective-permute-start | bytes 294920 | tf_op jit(solution)/shard_map/ppermute | solution.py:399
  43.0 4.3 %collective-permute-start.6 = (bf16[192,256]{1,0:T(8,128)(2,1)S(1)}, bf16[192,256]{1,0:T(8,128)(2,1)S(1)}, u32[]{:S(2)}, u32[]{:S(2)}) collective-permute-start(bf16[192,256]{1,0:T(8,128)(2,1)S(1)} %get-tuple-element.73), channel_id=1, source_target_pairs={{0,2},{1,3},{2,0},{3,1},{4,6},{5,7},{6,4},{7,5},{8,10},{9,11},{10,... | collective-permute-start | bytes 294920 | tf_op jit(solution)/shard_map/ppermute | solution.py:399
  44.0 5.6 %collective-permute-start.7 = (bf16[192,256]{1,0:T(8,128)(2,1)S(1)}, bf16[192,256]{1,0:T(8,128)(2,1)S(1)}, u32[]{:S(2)}, u32[]{:S(2)}) collective-permute-start(bf16[192,256]{1,0:T(8,128)(2,1)S(1)} %get-tuple-element.74), channel_id=1, source_target_pairs={{0,3},{1,2},{2,1},{3,0},{4,7},{5,6},{6,5},{7,4},{8,11},{9,10},{10,... | collective-permute-start | bytes 294920 | tf_op jit(solution)/shard_map/ppermute | solution.py:399
